TPU v7x, 256 devices: a whole 4x4x8 slice. The times are simulated.
256 devices in a mesh: depth: 32 (over z, x), tile: 8 (over y, core).
Axes of the slice: x: 4, y: 4, z: 8, core: 2. Of those that a mesh axis runs over, the one named last changes fastest.
Arguments:
- tidal: float32 [32, 3, 131072], P('depth', None, 'tile'), may hold values from -1.5 to 1.5
- plane_weight: float32 [32], P('depth'), may hold values from 0.2 to 1
- plane_step: float32 [32], P('depth'), may hold values from 0.2 to 0.6
- ray_angle: float32 [131072], P('tile'), may hold values from -3.140625 to 3.140625
- dest_tile: int32 [32, 1024, 1], P('depth', 'tile'), may hold values from 0 to 7; in each aligned block of 128 rows (0 to 127, 128 to 255, ..., all dimensions but the last counted through in order) at most 32 rows name the same one
- dest_segment: int32 [32, 1024], P('depth', 'tile'), may hold values from 0 to 255
- interp: bfloat16 [32, 1024, 128, 128], P('depth', 'tile'), may hold values from -0.5 to 0.5
Outputs:
- potential_adjoint: float32 [32, 16, 16384], P('depth', 'tile')
Inputs may be any that keep to these rules, and one draw needn't show every extreme that they name: `dest_tile`: in each plane, the 128 blocks of one strip name no strip more than 32 times, a bound that some block reaches.
All inputs are finite; a program needn't handle non-finite values.
Results may differ from a plain program's by a relative error of at most 0.003.
Values sent between devices are 32-bit elements; how exact they have to be, the bound alone decides.
A program may use at most 64 MiB of HBM per device.

v0:
```python
import jax
import jax.numpy as jnp
from jax import lax
from jax.sharding import PartitionSpec as P

ROWS = 2
COLS = 16384


def from_behind(value, axis, steps):
    count = lax.axis_size(axis)
    leading, last = (max(0, -steps), min(count, count - steps))
    return lax.ppermute(value, axis, [(source, source + steps) for source in range(leading, last)])


def padded_2(shard, sides, width):
    for axis, dim in sides:
        count, length = (lax.axis_size(axis), shard.shape[dim])
        up = [(i, (i + 1) % count) for i in range(count - 1)]
        down = [(j, i) for i, j in up]
        last = lax.slice_in_dim(shard, length - width, length, axis=dim)
        leading = lax.slice_in_dim(shard, 0, width, axis=dim)
        before = lax.ppermute(last, axis, up)
        after = lax.ppermute(leading, axis, down)
        shard = jnp.concatenate([before, shard, after], axis=dim)
    return shard


def column_part(field):
    padded = jnp.pad(field, ((0, 0), (0, 0), (1, 1)))
    return 0.5 * (padded[:, :, :-2] - padded[:, :, 2:])


def smooth_cols(field):
    padded = jnp.pad(field, ((0, 0), (0, 0), (1, 1)))
    return 0.25 * padded[:, :, :-2] + 0.5 * field + 0.25 * padded[:, :, 2:]


def per_device(tidal, plane_weight, plane_step, ray_angle, dest_tile, dest_segment, interp):
    planes_here = tidal.shape[0]
    n_tile = lax.axis_size("tile")
    n_depth = lax.axis_size("depth")
    blocks_here = interp.shape[1]
    width = interp.shape[2]
    slots = 2 * blocks_here // n_tile
    segments = ROWS * COLS // width
    jxx = tidal[:, 0]
    jxy = tidal[:, 1]
    jyy = tidal[:, 2]
    local_terms = jnp.stack(
        [
            -jnp.sum(plane_weight[:, None] * (jxx - jyy) * 0.5, axis=0),
            -jnp.sum(plane_weight[:, None] * jxy, axis=0),
        ]
    )
    shear = lax.psum(local_terms, "depth")
    cross = -shear[0] * jnp.sin(2.0 * ray_angle) + shear[1] * jnp.cos(2.0 * ray_angle)
    seed_state = jnp.stack(
        [
            cross * jnp.cos(ray_angle),
            cross * jnp.sin(ray_angle),
            jnp.zeros_like(cross),
            jnp.zeros_like(cross),
        ]
    )

    def sweep(top):
        xb_one, xb_two, tb_one, tb_two = (top[0], top[1], top[2], top[3])
        step_len = plane_step[0]
        tp_one = tb_one + step_len * xb_one
        tp_two = tb_two + step_len * xb_two
        adjoints = [jnp.stack([-tp_one, -tp_two])]
        new_one = xb_one - (jxx[0] * tp_one + jxy[0] * tp_two)
        new_two = xb_two - (jxy[0] * tp_one + jyy[0] * tp_two)
        return (jnp.stack([new_one, new_two, tp_one, tp_two]), jnp.stack(adjoints[::-1]))

    is_last = lax.axis_index("depth") == n_depth - 1

    def relay_step(turn, top):
        bottom, unused = sweep(top)
        incoming = from_behind(bottom, "depth", -1)
        return jnp.where(is_last, seed_state, incoming)

    top_state = lax.fori_loop(0, n_depth - 1, relay_step, seed_state)
    unused_state, deflection_bar = sweep(top_state)
    abar = deflection_bar.astype(jnp.bfloat16).reshape(planes_here, 2, blocks_here, width)
    contrib = jnp.einsum("pcbr,pbrk->pbck", abar, interp, preferred_element_type=jnp.float32)
    dest = dest_tile[:, :, 0]
    order_mask = jnp.arange(blocks_here)[None, :] < jnp.arange(blocks_here)[:, None]
    same_dest = dest[:, :, None] == dest[:, None, :]
    rank = jnp.sum(jnp.logical_and(same_dest, order_mask[None]), axis=2)
    slot = dest[0] * slots + rank[0]
    send_data = jnp.zeros((n_tile * slots, 2, width), jnp.float32).at[slot].set(contrib[0])
    send_ids = jnp.zeros((n_tile * slots,), jnp.int32).at[slot].set(dest_segment[0])
    got_data = lax.all_to_all(
        send_data.reshape(n_tile, slots, 2, width), "tile", split_axis=0, concat_axis=0, tiled=True
    )
    got_ids = lax.all_to_all(
        send_ids.reshape(n_tile, slots), "tile", split_axis=0, concat_axis=0, tiled=True
    )
    summed = (
        jnp.zeros((segments, 2, width), jnp.float32)
        .at[got_ids.reshape(-1)]
        .add(got_data.reshape(-1, 2, width))
    )
    plane_maps = [jnp.transpose(summed, (1, 0, 2)).reshape(2, ROWS, COLS)]
    maps = jnp.stack(plane_maps)
    ay_ext = padded_2(maps[:, 1], (("tile", 1),), 1)
    raw = column_part(maps[:, 0]) + 0.5 * (ay_ext[:, :-2, :] - ay_ext[:, 2:, :])
    raw_ext = padded_2(raw, (("tile", 1),), 1)
    rows_done = 0.25 * raw_ext[:, :-2, :] + 0.5 * raw_ext[:, 1:-1, :] + 0.25 * raw_ext[:, 2:, :]
    return smooth_cols(rows_done)


def solution(mesh):
    return jax.shard_map(
        per_device,
        mesh=mesh,
        in_specs=(
            P("depth", None, "tile"),
            P("depth"),
            P("depth"),
            P("tile"),
            P("depth", "tile", None),
            P("depth", "tile"),
            P("depth", "tile", None, None),
        ),
        out_specs=P("depth", "tile", None),
        check_vma=False,
    )
```

profile of v0, /device:TPU:103, one launch (start us, length us, event | category | flops | bytes accessed | tf_op | source)
XLA Modules:
  0.0 640.2 jit_solution(10379709504389961642)
XLA Ops:
  12.4 5.1 all-to-all-start
  19.2 129.9 %all-reduce.4.cloned.1.call-done = f32[2,16384]{1,0:T(2,128)} async-done(((f32[2,16384]{1,0:T(2,128)}), f32[2,16384]{1,0:T(2,128)}) %all-reduce.4.cloned.1.call-update) | async-done | bytes 131088 | tf_op jit(solution)/shard_map/psum | solution.py:56
  151.7 387.7 %while.10 = (s32[]{:T(128)}, f32[4,16384]{1,0:T(4,128)S(1)}, pred[]{:T(512)}, f32[1,1,16384]{2,1,0:T(1,128)S(1)}, f32[1]{0:T(128)}, /*index=5*/f32[1,1,16384]{2,...) while((s32[]{:T(128)}, f32[4,16384]{1,0:T(4,128)S(1)}, pred[]{:T(512)}, ...), condition=%wide.region_4.5_spmd, body=%wide.region_3.4_spmd.sunk | while | flops 458754 | bytes 3342474 | solution.py:84
  153.0 2.8 collective-permute-start
  155.8 7.6 %collective-permute-done = f32[4,16384]{1,0:T(4,128)S(1)} collective-permute-done((f32[4,16384]{1,0:T(4,128)S(1)}, f32[4,16384]{1,0:T(4,128)S(1)}, u32[]{:S(2)}, u32[]{:S(2)}) %collective-permute-start) | collective-permute-done | bytes 262176 | tf_op jit(solution)/shard_map/while/body/eval_jaxpr/ppermute | solution.py:13
  164.9 1.9 collective-permute-start
  166.8 8.5 %collective-permute-done = f32[4,16384]{1,0:T(4,128)S(1)} collective-permute-done((f32[4,16384]{1,0:T(4,128)S(1)}, f32[4,16384]{1,0:T(4,128)S(1)}, u32[]{:S(2)}, u32[]{:S(2)}) %collective-permute-start) | collective-permute-done | bytes 262176 | tf_op jit(solution)/shard_map/while/body/eval_jaxpr/ppermute | solution.py:13
  176.7 1.9 collective-permute-start
  178.7 8.5 %collective-permute-done = f32[4,16384]{1,0:T(4,128)S(1)} collective-permute-done((f32[4,16384]{1,0:T(4,128)S(1)}, f32[4,16384]{1,0:T(4,128)S(1)}, u32[]{:S(2)}, u32[]{:S(2)}) %collective-permute-start) | collective-permute-done | bytes 262176 | tf_op jit(solution)/shard_map/while/body/eval_jaxpr/ppermute | solution.py:13
  188.6 1.9 collective-permute-start
  190.5 8.5 %collective-permute-done = f32[4,16384]{1,0:T(4,128)S(1)} collective-permute-done((f32[4,16384]{1,0:T(4,128)S(1)}, f32[4,16384]{1,0:T(4,128)S(1)}, u32[]{:S(2)}, u32[]{:S(2)}) %collective-permute-start) | collective-permute-done | bytes 262176 | tf_op jit(solution)/shard_map/while/body/eval_jaxpr/ppermute | solution.py:13
  200.5 1.9 collective-permute-start
  202.4 8.7 %collective-permute-done = f32[4,16384]{1,0:T(4,128)S(1)} collective-permute-done((f32[4,16384]{1,0:T(4,128)S(1)}, f32[4,16384]{1,0:T(4,128)S(1)}, u32[]{:S(2)}, u32[]{:S(2)}) %collective-permute-start) | collective-permute-done | bytes 262176 | tf_op jit(solution)/shard_map/while/body/eval_jaxpr/ppermute | solution.py:13
  212.5 1.9 collective-permute-start
  214.5 9.9 %collective-permute-done = f32[4,16384]{1,0:T(4,128)S(1)} collective-permute-done((f32[4,16384]{1,0:T(4,128)S(1)}, f32[4,16384]{1,0:T(4,128)S(1)}, u32[]{:S(2)}, u32[]{:S(2)}) %collective-permute-start) | collective-permute-done | bytes 262176 | tf_op jit(solution)/shard_map/while/body/eval_jaxpr/ppermute | solution.py:13
  225.7 1.9 collective-permute-start
  227.7 11.0 %collective-permute-done = f32[4,16384]{1,0:T(4,128)S(1)} collective-permute-done((f32[4,16384]{1,0:T(4,128)S(1)}, f32[4,16384]{1,0:T(4,128)S(1)}, u32[]{:S(2)}, u32[]{:S(2)}) %collective-permute-start) | collective-permute-done | bytes 262176 | tf_op jit(solution)/shard_map/while/body/eval_jaxpr/ppermute | solution.py:13
  240.1 1.9 collective-permute-start
  242.0 10.8 %collective-permute-done = f32[4,16384]{1,0:T(4,128)S(1)} collective-permute-done((f32[4,16384]{1,0:T(4,128)S(1)}, f32[4,16384]{1,0:T(4,128)S(1)}, u32[]{:S(2)}, u32[]{:S(2)}) %collective-permute-start) | collective-permute-done | bytes 262176 | tf_op jit(solution)/shard_map/while/body/eval_jaxpr/ppermute | solution.py:13
  254.2 1.9 collective-permute-start
  256.1 9.9 %collective-permute-done = f32[4,16384]{1,0:T(4,128)S(1)} collective-permute-done((f32[4,16384]{1,0:T(4,128)S(1)}, f32[4,16384]{1,0:T(4,128)S(1)}, u32[]{:S(2)}, u32[]{:S(2)}) %collective-permute-start) | collective-permute-done | bytes 262176 | tf_op jit(solution)/shard_map/while/body/eval_jaxpr/ppermute | solution.py:13
  267.5 1.9 collective-permute-start
  269.4 9.1 %collective-permute-done = f32[4,16384]{1,0:T(4,128)S(1)} collective-permute-done((f32[4,16384]{1,0:T(4,128)S(1)}, f32[4,16384]{1,0:T(4,128)S(1)}, u32[]{:S(2)}, u32[]{:S(2)}) %collective-permute-start) | collective-permute-done | bytes 262176 | tf_op jit(solution)/shard_map/while/body/eval_jaxpr/ppermute | solution.py:13
  279.9 1.9 collective-permute-start
  281.8 8.5 %collective-permute-done = f32[4,16384]{1,0:T(4,128)S(1)} collective-permute-done((f32[4,16384]{1,0:T(4,128)S(1)}, f32[4,16384]{1,0:T(4,128)S(1)}, u32[]{:S(2)}, u32[]{:S(2)}) %collective-permute-start) | collective-permute-done | bytes 262176 | tf_op jit(solution)/shard_map/while/body/eval_jaxpr/ppermute | solution.py:13
  291.8 1.9 collective-permute-start
  293.7 8.5 %collective-permute-done = f32[4,16384]{1,0:T(4,128)S(1)} collective-permute-done((f32[4,16384]{1,0:T(4,128)S(1)}, f32[4,16384]{1,0:T(4,128)S(1)}, u32[]{:S(2)}, u32[]{:S(2)}) %collective-permute-start) | collective-permute-done | bytes 262176 | tf_op jit(solution)/shard_map/while/body/eval_jaxpr/ppermute | solution.py:13
  303.6 1.9 collective-permute-start
  305.6 8.5 %collective-permute-done = f32[4,16384]{1,0:T(4,128)S(1)} collective-permute-done((f32[4,16384]{1,0:T(4,128)S(1)}, f32[4,16384]{1,0:T(4,128)S(1)}, u32[]{:S(2)}, u32[]{:S(2)}) %collective-permute-start) | collective-permute-done | bytes 262176 | tf_op jit(solution)/shard_map/while/body/eval_jaxpr/ppermute | solution.py:13
  315.5 1.9 collective-permute-start
  317.4 8.5 %collective-permute-done = f32[4,16384]{1,0:T(4,128)S(1)} collective-permute-done((f32[4,16384]{1,0:T(4,128)S(1)}, f32[4,16384]{1,0:T(4,128)S(1)}, u32[]{:S(2)}, u32[]{:S(2)}) %collective-permute-start) | collective-permute-done | bytes 262176 | tf_op jit(solution)/shard_map/while/body/eval_jaxpr/ppermute | solution.py:13
  327.4 1.9 collective-permute-start
  329.3 8.5 %collective-permute-done = f32[4,16384]{1,0:T(4,128)S(1)} collective-permute-done((f32[4,16384]{1,0:T(4,128)S(1)}, f32[4,16384]{1,0:T(4,128)S(1)}, u32[]{:S(2)}, u32[]{:S(2)}) %collective-permute-start) | collective-permute-done | bytes 262176 | tf_op jit(solution)/shard_map/while/body/eval_jaxpr/ppermute | solution.py:13
  339.2 1.9 collective-permute-start
  341.1 8.5 %collective-permute-done = f32[4,16384]{1,0:T(4,128)S(1)} collective-permute-done((f32[4,16384]{1,0:T(4,128)S(1)}, f32[4,16384]{1,0:T(4,128)S(1)}, u32[]{:S(2)}, u32[]{:S(2)}) %collective-permute-start) | collective-permute-done | bytes 262176 | tf_op jit(solution)/shard_map/while/body/eval_jaxpr/ppermute | solution.py:13
  351.1 1.9 collective-permute-start
  353.0 8.6 %collective-permute-done = f32[4,16384]{1,0:T(4,128)S(1)} collective-permute-done((f32[4,16384]{1,0:T(4,128)S(1)}, f32[4,16384]{1,0:T(4,128)S(1)}, u32[]{:S(2)}, u32[]{:S(2)}) %collective-permute-start) | collective-permute-done | bytes 262176 | tf_op jit(solution)/shard_map/while/body/eval_jaxpr/ppermute | solution.py:13
  365.0 9.8 %collective-permute-done = f32[4,16384]{1,0:T(4,128)S(1)} collective-permute-done((f32[4,16384]{1,0:T(4,128)S(1)}, f32[4,16384]{1,0:T(4,128)S(1)}, u32[]{:S(2)}, u32[]{:S(2)}) %collective-permute-start) | collective-permute-done | bytes 262176 | tf_op jit(solution)/shard_map/while/body/eval_jaxpr/ppermute | solution.py:13
  376.1 1.9 collective-permute-start
  378.1 10.9 %collective-permute-done = f32[4,16384]{1,0:T(4,128)S(1)} collective-permute-done((f32[4,16384]{1,0:T(4,128)S(1)}, f32[4,16384]{1,0:T(4,128)S(1)}, u32[]{:S(2)}, u32[]{:S(2)}) %collective-permute-start) | collective-permute-done | bytes 262176 | tf_op jit(solution)/shard_map/while/body/eval_jaxpr/ppermute | solution.py:13
  392.3 10.9 %collective-permute-done = f32[4,16384]{1,0:T(4,128)S(1)} collective-permute-done((f32[4,16384]{1,0:T(4,128)S(1)}, f32[4,16384]{1,0:T(4,128)S(1)}, u32[]{:S(2)}, u32[]{:S(2)}) %collective-permute-start) | collective-permute-done | bytes 262176 | tf_op jit(solution)/shard_map/while/body/eval_jaxpr/ppermute | solution.py:13
  406.6 10.0 %collective-permute-done = f32[4,16384]{1,0:T(4,128)S(1)} collective-permute-done((f32[4,16384]{1,0:T(4,128)S(1)}, f32[4,16384]{1,0:T(4,128)S(1)}, u32[]{:S(2)}, u32[]{:S(2)}) %collective-permute-start) | collective-permute-done | bytes 262176 | tf_op jit(solution)/shard_map/while/body/eval_jaxpr/ppermute | solution.py:13
  419.9 9.2 %collective-permute-done = f32[4,16384]{1,0:T(4,128)S(1)} collective-permute-done((f32[4,16384]{1,0:T(4,128)S(1)}, f32[4,16384]{1,0:T(4,128)S(1)}, u32[]{:S(2)}, u32[]{:S(2)}) %collective-permute-start) | collective-permute-done | bytes 262176 | tf_op jit(solution)/shard_map/while/body/eval_jaxpr/ppermute | solution.py:13
  432.5 8.5 %collective-permute-done = f32[4,16384]{1,0:T(4,128)S(1)} collective-permute-done((f32[4,16384]{1,0:T(4,128)S(1)}, f32[4,16384]{1,0:T(4,128)S(1)}, u32[]{:S(2)}, u32[]{:S(2)}) %collective-permute-start) | collective-permute-done | bytes 262176 | tf_op jit(solution)/shard_map/while/body/eval_jaxpr/ppermute | solution.py:13
  442.4 1.9 collective-permute-start
  444.3 8.5 %collective-permute-done = f32[4,16384]{1,0:T(4,128)S(1)} collective-permute-done((f32[4,16384]{1,0:T(4,128)S(1)}, f32[4,16384]{1,0:T(4,128)S(1)}, u32[]{:S(2)}, u32[]{:S(2)}) %collective-permute-start) | collective-permute-done | bytes 262176 | tf_op jit(solution)/shard_map/while/body/eval_jaxpr/ppermute | solution.py:13
  456.2 8.5 %collective-permute-done = f32[4,16384]{1,0:T(4,128)S(1)} collective-permute-done((f32[4,16384]{1,0:T(4,128)S(1)}, f32[4,16384]{1,0:T(4,128)S(1)}, u32[]{:S(2)}, u32[]{:S(2)}) %collective-permute-start) | collective-permute-done | bytes 262176 | tf_op jit(solution)/shard_map/while/body/eval_jaxpr/ppermute | solution.py:13
  468.0 8.5 %collective-permute-done = f32[4,16384]{1,0:T(4,128)S(1)} collective-permute-done((f32[4,16384]{1,0:T(4,128)S(1)}, f32[4,16384]{1,0:T(4,128)S(1)}, u32[]{:S(2)}, u32[]{:S(2)}) %collective-permute-start) | collective-permute-done | bytes 262176 | tf_op jit(solution)/shard_map/while/body/eval_jaxpr/ppermute | solution.py:13
  478.0 1.9 collective-permute-start
  479.9 8.5 %collective-permute-done = f32[4,16384]{1,0:T(4,128)S(1)} collective-permute-done((f32[4,16384]{1,0:T(4,128)S(1)}, f32[4,16384]{1,0:T(4,128)S(1)}, u32[]{:S(2)}, u32[]{:S(2)}) %collective-permute-start) | collective-permute-done | bytes 262176 | tf_op jit(solution)/shard_map/while/body/eval_jaxpr/ppermute | solution.py:13
  491.8 8.5 %collective-permute-done = f32[4,16384]{1,0:T(4,128)S(1)} collective-permute-done((f32[4,16384]{1,0:T(4,128)S(1)}, f32[4,16384]{1,0:T(4,128)S(1)}, u32[]{:S(2)}, u32[]{:S(2)}) %collective-permute-start) | collective-permute-done | bytes 262176 | tf_op jit(solution)/shard_map/while/body/eval_jaxpr/ppermute | solution.py:13
  503.6 8.5 %collective-permute-done = f32[4,16384]{1,0:T(4,128)S(1)} collective-permute-done((f32[4,16384]{1,0:T(4,128)S(1)}, f32[4,16384]{1,0:T(4,128)S(1)}, u32[]{:S(2)}, u32[]{:S(2)}) %collective-permute-start) | collective-permute-done | bytes 262176 | tf_op jit(solution)/shard_map/while/body/eval_jaxpr/ppermute | solution.py:13
  515.5 9.6 %collective-permute-done = f32[4,16384]{1,0:T(4,128)S(1)} collective-permute-done((f32[4,16384]{1,0:T(4,128)S(1)}, f32[4,16384]{1,0:T(4,128)S(1)}, u32[]{:S(2)}, u32[]{:S(2)}) %collective-permute-start) | collective-permute-done | bytes 262176 | tf_op jit(solution)/shard_map/while/body/eval_jaxpr/ppermute | solution.py:13
  528.5 10.8 %collective-permute-done = f32[4,16384]{1,0:T(4,128)S(1)} collective-permute-done((f32[4,16384]{1,0:T(4,128)S(1)}, f32[4,16384]{1,0:T(4,128)S(1)}, u32[]{:S(2)}, u32[]{:S(2)}) %collective-permute-start) | collective-permute-done | bytes 262176 | tf_op jit(solution)/shard_map/while/body/eval_jaxpr/ppermute | solution.py:13
  539.6 3.4 fusion.4
  543.8 12.5 %scatter_fusion = f32[256,2,128]{2,1,0:T(2,128)} fusion(f32[256,2,128]{2,1,0:T(2,128)} %broadcast.154.clone, s32[128]{0:T(128)S(1)} %fusion.14, f32[128,2,128]{2,1,0:T(2,128)S(1)} %fusion.4), kind=kCustom, calls=%fused_computation.1 | custom fusion | bytes 393728 | tf_op jit(solution)/shard_map/scatter | solution.py:93
  556.2 43.5 %all-to-all-start.1 = ((f32[8,32,2,128]{3,2,1,0:T(2,128)}), f32[8,32,2,128]{3,2,1,0:T(2,128)S(1)}, u32[]{:S(2)}, u32[]{:S(2)}) async-start(f32[8,32,2,128]{3,2,1,0:T(2,128)} %bitcast.21), calls=%async_computation.1 | async-start | bytes 524288 | tf_op jit(solution)/shard_map/all_to_all | solution.py:95
  601.0 5.2 all-to-all-done.1
  606.3 8.9 %scatter_fusion.1 = f32[256,2,128]{2,1,0:T(2,128)S(1)} fusion(f32[256,2,128]{2,1,0:T(2,128)S(1)} %broadcast.154, s32[256]{0:T(256)S(1)} %bitcast.85, f32[256,2,128]{2,1,0:T(2,128)S(1)} %bitcast.80), kind=kCustom, calls=%fused_computation.2 | custom fusion | flops 65536 | bytes 787456 | tf_op jit(solution)/shard_map/scatter-add | solution.py:104
  615.5 3.0 collective-permute-start.1
  618.5 1.9 collective-permute-start.2
  620.4 3.6 collective-permute-done.2
  626.5 2.4 collective-permute-start.4
  629.0 3.2 collective-permute-done.4
  (169 shorter events, 79.2 us)
Async XLA Ops:
  6.5 142.5 %all-reduce.4.cloned.1.call-start = ((), (), s32[]{:S(2)}) async-start(), calls=%async_computation.2 | async-start | bytes 262144 | tf_op jit(solution)/shard_map/psum | solution.py:56
  12.4 543.9 %all-to-all-start = ((s32[8,1,32]{2,1,0:T(1,128)}), s32[8,1,32]{2,1,0:T(1,128)S(1)}, u32[]{:S(2)}, u32[]{:S(2)}) async-start(s32[8,1,32]{2,1,0:T(1,128)} %all_to_all.9), calls=%async_computation | async-start | bytes 8192 | tf_op jit(solution)/shard_map/all_to_all | solution.py:98
  153.0 10.4 %collective-permute-start = (f32[4,16384]{1,0:T(4,128)S(1)}, f32[4,16384]{1,0:T(4,128)S(1)}, u32[]{:S(2)}, u32[]{:S(2)}) collective-permute-start(f32[4,16384]{1,0:T(4,128)S(1)} %pad_maximum_fusion.7), channel_id=1, source_target_pairs={{8,0},{16,8},{24,16},{32,24},{40,32},{48,40},{56,48},{64,56},{72,6... | collective-permute-start | bytes 786440 | tf_op jit(solution)/shard_map/while/body/eval_jaxpr/ppermute | solution.py:13
  164.9 10.4 %collective-permute-start = (f32[4,16384]{1,0:T(4,128)S(1)}, f32[4,16384]{1,0:T(4,128)S(1)}, u32[]{:S(2)}, u32[]{:S(2)}) collective-permute-start(f32[4,16384]{1,0:T(4,128)S(1)} %pad_maximum_fusion.7), channel_id=1, source_target_pairs={{8,0},{16,8},{24,16},{32,24},{40,32},{48,40},{56,48},{64,56},{72,6... | collective-permute-start | bytes 786440 | tf_op jit(solution)/shard_map/while/body/eval_jaxpr/ppermute | solution.py:13
  176.7 10.4 %collective-permute-start = (f32[4,16384]{1,0:T(4,128)S(1)}, f32[4,16384]{1,0:T(4,128)S(1)}, u32[]{:S(2)}, u32[]{:S(2)}) collective-permute-start(f32[4,16384]{1,0:T(4,128)S(1)} %pad_maximum_fusion.7), channel_id=1, source_target_pairs={{8,0},{16,8},{24,16},{32,24},{40,32},{48,40},{56,48},{64,56},{72,6... | collective-permute-start | bytes 786440 | tf_op jit(solution)/shard_map/while/body/eval_jaxpr/ppermute | solution.py:13
  188.6 10.4 %collective-permute-start = (f32[4,16384]{1,0:T(4,128)S(1)}, f32[4,16384]{1,0:T(4,128)S(1)}, u32[]{:S(2)}, u32[]{:S(2)}) collective-permute-start(f32[4,16384]{1,0:T(4,128)S(1)} %pad_maximum_fusion.7), channel_id=1, source_target_pairs={{8,0},{16,8},{24,16},{32,24},{40,32},{48,40},{56,48},{64,56},{72,6... | collective-permute-start | bytes 786440 | tf_op jit(solution)/shard_map/while/body/eval_jaxpr/ppermute | solution.py:13
  200.5 10.6 %collective-permute-start = (f32[4,16384]{1,0:T(4,128)S(1)}, f32[4,16384]{1,0:T(4,128)S(1)}, u32[]{:S(2)}, u32[]{:S(2)}) collective-permute-start(f32[4,16384]{1,0:T(4,128)S(1)} %pad_maximum_fusion.7), channel_id=1, source_target_pairs={{8,0},{16,8},{24,16},{32,24},{40,32},{48,40},{56,48},{64,56},{72,6... | collective-permute-start | bytes 786440 | tf_op jit(solution)/shard_map/while/body/eval_jaxpr/ppermute | solution.py:13
  212.5 11.8 %collective-permute-start = (f32[4,16384]{1,0:T(4,128)S(1)}, f32[4,16384]{1,0:T(4,128)S(1)}, u32[]{:S(2)}, u32[]{:S(2)}) collective-permute-start(f32[4,16384]{1,0:T(4,128)S(1)} %pad_maximum_fusion.7), channel_id=1, source_target_pairs={{8,0},{16,8},{24,16},{32,24},{40,32},{48,40},{56,48},{64,56},{72,6... | collective-permute-start | bytes 786440 | tf_op jit(solution)/shard_map/while/body/eval_jaxpr/ppermute | solution.py:13
  225.7 12.9 %collective-permute-start = (f32[4,16384]{1,0:T(4,128)S(1)}, f32[4,16384]{1,0:T(4,128)S(1)}, u32[]{:S(2)}, u32[]{:S(2)}) collective-permute-start(f32[4,16384]{1,0:T(4,128)S(1)} %pad_maximum_fusion.7), channel_id=1, source_target_pairs={{8,0},{16,8},{24,16},{32,24},{40,32},{48,40},{56,48},{64,56},{72,6... | collective-permute-start | bytes 786440 | tf_op jit(solution)/shard_map/while/body/eval_jaxpr/ppermute | solution.py:13
  240.1 12.7 %collective-permute-start = (f32[4,16384]{1,0:T(4,128)S(1)}, f32[4,16384]{1,0:T(4,128)S(1)}, u32[]{:S(2)}, u32[]{:S(2)}) collective-permute-start(f32[4,16384]{1,0:T(4,128)S(1)} %pad_maximum_fusion.7), channel_id=1, source_target_pairs={{8,0},{16,8},{24,16},{32,24},{40,32},{48,40},{56,48},{64,56},{72,6... | collective-permute-start | bytes 786440 | tf_op jit(solution)/shard_map/while/body/eval_jaxpr/ppermute | solution.py:13
  254.2 11.9 %collective-permute-start = (f32[4,16384]{1,0:T(4,128)S(1)}, f32[4,16384]{1,0:T(4,128)S(1)}, u32[]{:S(2)}, u32[]{:S(2)}) collective-permute-start(f32[4,16384]{1,0:T(4,128)S(1)} %pad_maximum_fusion.7), channel_id=1, source_target_pairs={{8,0},{16,8},{24,16},{32,24},{40,32},{48,40},{56,48},{64,56},{72,6... | collective-permute-start | bytes 786440 | tf_op jit(solution)/shard_map/while/body/eval_jaxpr/ppermute | solution.py:13
  267.5 11.0 %collective-permute-start = (f32[4,16384]{1,0:T(4,128)S(1)}, f32[4,16384]{1,0:T(4,128)S(1)}, u32[]{:S(2)}, u32[]{:S(2)}) collective-permute-start(f32[4,16384]{1,0:T(4,128)S(1)} %pad_maximum_fusion.7), channel_id=1, source_target_pairs={{8,0},{16,8},{24,16},{32,24},{40,32},{48,40},{56,48},{64,56},{72,6... | collective-permute-start | bytes 786440 | tf_op jit(solution)/shard_map/while/body/eval_jaxpr/ppermute | solution.py:13
  279.9 10.4 %collective-permute-start = (f32[4,16384]{1,0:T(4,128)S(1)}, f32[4,16384]{1,0:T(4,128)S(1)}, u32[]{:S(2)}, u32[]{:S(2)}) collective-permute-start(f32[4,16384]{1,0:T(4,128)S(1)} %pad_maximum_fusion.7), channel_id=1, source_target_pairs={{8,0},{16,8},{24,16},{32,24},{40,32},{48,40},{56,48},{64,56},{72,6... | collective-permute-start | bytes 786440 | tf_op jit(solution)/shard_map/while/body/eval_jaxpr/ppermute | solution.py:13
  291.8 10.4 %collective-permute-start = (f32[4,16384]{1,0:T(4,128)S(1)}, f32[4,16384]{1,0:T(4,128)S(1)}, u32[]{:S(2)}, u32[]{:S(2)}) collective-permute-start(f32[4,16384]{1,0:T(4,128)S(1)} %pad_maximum_fusion.7), channel_id=1, source_target_pairs={{8,0},{16,8},{24,16},{32,24},{40,32},{48,40},{56,48},{64,56},{72,6... | collective-permute-start | bytes 786440 | tf_op jit(solution)/shard_map/while/body/eval_jaxpr/ppermute | solution.py:13
  303.6 10.4 %collective-permute-start = (f32[4,16384]{1,0:T(4,128)S(1)}, f32[4,16384]{1,0:T(4,128)S(1)}, u32[]{:S(2)}, u32[]{:S(2)}) collective-permute-start(f32[4,16384]{1,0:T(4,128)S(1)} %pad_maximum_fusion.7), channel_id=1, source_target_pairs={{8,0},{16,8},{24,16},{32,24},{40,32},{48,40},{56,48},{64,56},{72,6... | collective-permute-start | bytes 786440 | tf_op jit(solution)/shard_map/while/body/eval_jaxpr/ppermute | solution.py:13
  315.5 10.4 %collective-permute-start = (f32[4,16384]{1,0:T(4,128)S(1)}, f32[4,16384]{1,0:T(4,128)S(1)}, u32[]{:S(2)}, u32[]{:S(2)}) collective-permute-start(f32[4,16384]{1,0:T(4,128)S(1)} %pad_maximum_fusion.7), channel_id=1, source_target_pairs={{8,0},{16,8},{24,16},{32,24},{40,32},{48,40},{56,48},{64,56},{72,6... | collective-permute-start | bytes 786440 | tf_op jit(solution)/shard_map/while/body/eval_jaxpr/ppermute | solution.py:13
  327.4 10.4 %collective-permute-start = (f32[4,16384]{1,0:T(4,128)S(1)}, f32[4,16384]{1,0:T(4,128)S(1)}, u32[]{:S(2)}, u32[]{:S(2)}) collective-permute-start(f32[4,16384]{1,0:T(4,128)S(1)} %pad_maximum_fusion.7), channel_id=1, source_target_pairs={{8,0},{16,8},{24,16},{32,24},{40,32},{48,40},{56,48},{64,56},{72,6... | collective-permute-start | bytes 786440 | tf_op jit(solution)/shard_map/while/body/eval_jaxpr/ppermute | solution.py:13
  339.2 10.4 %collective-permute-start = (f32[4,16384]{1,0:T(4,128)S(1)}, f32[4,16384]{1,0:T(4,128)S(1)}, u32[]{:S(2)}, u32[]{:S(2)}) collective-permute-start(f32[4,16384]{1,0:T(4,128)S(1)} %pad_maximum_fusion.7), channel_id=1, source_target_pairs={{8,0},{16,8},{24,16},{32,24},{40,32},{48,40},{56,48},{64,56},{72,6... | collective-permute-start | bytes 786440 | tf_op jit(solution)/shard_map/while/body/eval_jaxpr/ppermute | solution.py:13
  351.1 10.5 %collective-permute-start = (f32[4,16384]{1,0:T(4,128)S(1)}, f32[4,16384]{1,0:T(4,128)S(1)}, u32[]{:S(2)}, u32[]{:S(2)}) collective-permute-start(f32[4,16384]{1,0:T(4,128)S(1)} %pad_maximum_fusion.7), channel_id=1, source_target_pairs={{8,0},{16,8},{24,16},{32,24},{40,32},{48,40},{56,48},{64,56},{72,6... | collective-permute-start | bytes 786440 | tf_op jit(solution)/shard_map/while/body/eval_jaxpr/ppermute | solution.py:13
  363.0 11.7 %collective-permute-start = (f32[4,16384]{1,0:T(4,128)S(1)}, f32[4,16384]{1,0:T(4,128)S(1)}, u32[]{:S(2)}, u32[]{:S(2)}) collective-permute-start(f32[4,16384]{1,0:T(4,128)S(1)} %pad_maximum_fusion.7), channel_id=1, source_target_pairs={{8,0},{16,8},{24,16},{32,24},{40,32},{48,40},{56,48},{64,56},{72,6... | collective-permute-start | bytes 786440 | tf_op jit(solution)/shard_map/while/body/eval_jaxpr/ppermute | solution.py:13
  376.1 12.8 %collective-permute-start = (f32[4,16384]{1,0:T(4,128)S(1)}, f32[4,16384]{1,0:T(4,128)S(1)}, u32[]{:S(2)}, u32[]{:S(2)}) collective-permute-start(f32[4,16384]{1,0:T(4,128)S(1)} %pad_maximum_fusion.7), channel_id=1, source_target_pairs={{8,0},{16,8},{24,16},{32,24},{40,32},{48,40},{56,48},{64,56},{72,6... | collective-permute-start | bytes 786440 | tf_op jit(solution)/shard_map/while/body/eval_jaxpr/ppermute | solution.py:13
  390.4 12.8 %collective-permute-start = (f32[4,16384]{1,0:T(4,128)S(1)}, f32[4,16384]{1,0:T(4,128)S(1)}, u32[]{:S(2)}, u32[]{:S(2)}) collective-permute-start(f32[4,16384]{1,0:T(4,128)S(1)} %pad_maximum_fusion.7), channel_id=1, source_target_pairs={{8,0},{16,8},{24,16},{32,24},{40,32},{48,40},{56,48},{64,56},{72,6... | collective-permute-start | bytes 786440 | tf_op jit(solution)/shard_map/while/body/eval_jaxpr/ppermute | solution.py:13
  404.6 12.0 %collective-permute-start = (f32[4,16384]{1,0:T(4,128)S(1)}, f32[4,16384]{1,0:T(4,128)S(1)}, u32[]{:S(2)}, u32[]{:S(2)}) collective-permute-start(f32[4,16384]{1,0:T(4,128)S(1)} %pad_maximum_fusion.7), channel_id=1, source_target_pairs={{8,0},{16,8},{24,16},{32,24},{40,32},{48,40},{56,48},{64,56},{72,6... | collective-permute-start | bytes 786440 | tf_op jit(solution)/shard_map/while/body/eval_jaxpr/ppermute | solution.py:13
  418.0 11.1 %collective-permute-start = (f32[4,16384]{1,0:T(4,128)S(1)}, f32[4,16384]{1,0:T(4,128)S(1)}, u32[]{:S(2)}, u32[]{:S(2)}) collective-permute-start(f32[4,16384]{1,0:T(4,128)S(1)} %pad_maximum_fusion.7), channel_id=1, source_target_pairs={{8,0},{16,8},{24,16},{32,24},{40,32},{48,40},{56,48},{64,56},{72,6... | collective-permute-start | bytes 786440 | tf_op jit(solution)/shard_map/while/body/eval_jaxpr/ppermute | solution.py:13
  430.5 10.4 %collective-permute-start = (f32[4,16384]{1,0:T(4,128)S(1)}, f32[4,16384]{1,0:T(4,128)S(1)}, u32[]{:S(2)}, u32[]{:S(2)}) collective-permute-start(f32[4,16384]{1,0:T(4,128)S(1)} %pad_maximum_fusion.7), channel_id=1, source_target_pairs={{8,0},{16,8},{24,16},{32,24},{40,32},{48,40},{56,48},{64,56},{72,6... | collective-permute-start | bytes 786440 | tf_op jit(solution)/shard_map/while/body/eval_jaxpr/ppermute | solution.py:13
  442.4 10.4 %collective-permute-start = (f32[4,16384]{1,0:T(4,128)S(1)}, f32[4,16384]{1,0:T(4,128)S(1)}, u32[]{:S(2)}, u32[]{:S(2)}) collective-permute-start(f32[4,16384]{1,0:T(4,128)S(1)} %pad_maximum_fusion.7), channel_id=1, source_target_pairs={{8,0},{16,8},{24,16},{32,24},{40,32},{48,40},{56,48},{64,56},{72,6... | collective-permute-start | bytes 786440 | tf_op jit(solution)/shard_map/while/body/eval_jaxpr/ppermute | solution.py:13
  454.3 10.4 %collective-permute-start = (f32[4,16384]{1,0:T(4,128)S(1)}, f32[4,16384]{1,0:T(4,128)S(1)}, u32[]{:S(2)}, u32[]{:S(2)}) collective-permute-start(f32[4,16384]{1,0:T(4,128)S(1)} %pad_maximum_fusion.7), channel_id=1, source_target_pairs={{8,0},{16,8},{24,16},{32,24},{40,32},{48,40},{56,48},{64,56},{72,6... | collective-permute-start | bytes 786440 | tf_op jit(solution)/shard_map/while/body/eval_jaxpr/ppermute | solution.py:13
  466.1 10.4 %collective-permute-start = (f32[4,16384]{1,0:T(4,128)S(1)}, f32[4,16384]{1,0:T(4,128)S(1)}, u32[]{:S(2)}, u32[]{:S(2)}) collective-permute-start(f32[4,16384]{1,0:T(4,128)S(1)} %pad_maximum_fusion.7), channel_id=1, source_target_pairs={{8,0},{16,8},{24,16},{32,24},{40,32},{48,40},{56,48},{64,56},{72,6... | collective-permute-start | bytes 786440 | tf_op jit(solution)/shard_map/while/body/eval_jaxpr/ppermute | solution.py:13
  478.0 10.4 %collective-permute-start = (f32[4,16384]{1,0:T(4,128)S(1)}, f32[4,16384]{1,0:T(4,128)S(1)}, u32[]{:S(2)}, u32[]{:S(2)}) collective-permute-start(f32[4,16384]{1,0:T(4,128)S(1)} %pad_maximum_fusion.7), channel_id=1, source_target_pairs={{8,0},{16,8},{24,16},{32,24},{40,32},{48,40},{56,48},{64,56},{72,6... | collective-permute-start | bytes 786440 | tf_op jit(solution)/shard_map/while/body/eval_jaxpr/ppermute | solution.py:13
  489.8 10.4 %collective-permute-start = (f32[4,16384]{1,0:T(4,128)S(1)}, f32[4,16384]{1,0:T(4,128)S(1)}, u32[]{:S(2)}, u32[]{:S(2)}) collective-permute-start(f32[4,16384]{1,0:T(4,128)S(1)} %pad_maximum_fusion.7), channel_id=1, source_target_pairs={{8,0},{16,8},{24,16},{32,24},{40,32},{48,40},{56,48},{64,56},{72,6... | collective-permute-start | bytes 786440 | tf_op jit(solution)/shard_map/while/body/eval_jaxpr/ppermute | solution.py:13
  501.7 10.4 %collective-permute-start = (f32[4,16384]{1,0:T(4,128)S(1)}, f32[4,16384]{1,0:T(4,128)S(1)}, u32[]{:S(2)}, u32[]{:S(2)}) collective-permute-start(f32[4,16384]{1,0:T(4,128)S(1)} %pad_maximum_fusion.7), channel_id=1, source_target_pairs={{8,0},{16,8},{24,16},{32,24},{40,32},{48,40},{56,48},{64,56},{72,6... | collective-permute-start | bytes 786440 | tf_op jit(solution)/shard_map/while/body/eval_jaxpr/ppermute | solution.py:13
  513.6 11.6 %collective-permute-start = (f32[4,16384]{1,0:T(4,128)S(1)}, f32[4,16384]{1,0:T(4,128)S(1)}, u32[]{:S(2)}, u32[]{:S(2)}) collective-permute-start(f32[4,16384]{1,0:T(4,128)S(1)} %pad_maximum_fusion.7), channel_id=1, source_target_pairs={{8,0},{16,8},{24,16},{32,24},{40,32},{48,40},{56,48},{64,56},{72,6... | collective-permute-start | bytes 786440 | tf_op jit(solution)/shard_map/while/body/eval_jaxpr/ppermute | solution.py:13
  526.6 12.7 %collective-permute-start = (f32[4,16384]{1,0:T(4,128)S(1)}, f32[4,16384]{1,0:T(4,128)S(1)}, u32[]{:S(2)}, u32[]{:S(2)}) collective-permute-start(f32[4,16384]{1,0:T(4,128)S(1)} %pad_maximum_fusion.7), channel_id=1, source_target_pairs={{8,0},{16,8},{24,16},{32,24},{40,32},{48,40},{56,48},{64,56},{72,6... | collective-permute-start | bytes 786440 | tf_op jit(solution)/shard_map/while/body/eval_jaxpr/ppermute | solution.py:13
  556.2 50.0 %all-to-all-start.1 = ((f32[8,32,2,128]{3,2,1,0:T(2,128)}), f32[8,32,2,128]{3,2,1,0:T(2,128)S(1)}, u32[]{:S(2)}, u32[]{:S(2)}) async-start(f32[8,32,2,128]{3,2,1,0:T(2,128)} %bitcast.21), calls=%async_computation.1 | async-start | bytes 524288 | tf_op jit(solution)/shard_map/all_to_all | solution.py:95
  615.5 5.0 collective-permute-start.1
  618.5 5.6 collective-permute-start.2
  624.6 4.3 collective-permute-start.3
  626.5 5.6 collective-permute-start.4
Sparse Core Ops, SparseCore 0:
  10.8 138.2 all-reduce.3
where the time goes:
time: 642 us; the launch traced here: 640 us
  waiting for transfers between devices  425 us (66%)
  starting transfers between devices  118 us (18%)
  other arithmetic  60.3 us (9%)
  local copies, waits for them, and re-layouts  17.1 us (3%)
  between operations  14.9 us (2%)
    ppermute x31, waiting for transfers between devices, from_behind(): lax.ppermute(value, axis, [(source, source + steps) for source in range(l...  283 us
    psum x1, waiting for transfers between devices, per_device(): shear = lax.psum(local_terms, 'depth')  130 us
    ppermute x31, starting transfers between devices, from_behind(): lax.ppermute(value, axis, [(source, source + steps) for source in range(l...  60.4 us
    all_to_all x1, starting transfers between devices, per_device(): lax.all_to_all(send_data.reshape(n_tile, slots, 2, width), 'tile', split_...  43.5 us
    sub x31, other arithmetic, sweep(): new_one = xb_one - (jxx[0] * tp_one + jxy[0] * tp_two)  27.6 us
  transfers between devices with their start and end apart: 38, of which 35 were waited for; matrix products, arithmetic and copies ran while one was open for 11% of the time, Pallas kernels for 0%

commit v1 on v0

v1 whole, which is shorter than its diff:
```python
import jax
import jax.numpy as jnp
from jax import lax
from jax.experimental import pallas as pl
from jax.experimental.pallas import tpu as pltpu
from jax.sharding import PartitionSpec as P

ROWS = 2
COLS = 16384
HI = lax.Precision.HIGHEST


def all_to_all(value, axis):
    return lax.all_to_all(value, axis, split_axis=0, concat_axis=0, tiled=True)


def shift_cols(field):
    padded = jnp.pad(field, ((0, 0), (1, 1)))
    return padded[:, :-2], padded[:, 2:]


def sweep_kernel(planes, trig, adjoints):
    count = planes.shape[0]
    g_one = jnp.zeros(planes.shape[2:], jnp.float32)
    g_two = jnp.zeros(planes.shape[2:], jnp.float32)
    for plane in range(count):
        weight = planes[plane, 3, 0:1]
        g_one -= weight * (planes[plane, 0] - planes[plane, 2]) * 0.5
        g_two -= weight * planes[plane, 1]
    cross = -g_one * trig[0] + g_two * trig[1]
    xb_one, xb_two = cross * trig[3], cross * trig[2]
    tb_one = tb_two = jnp.zeros_like(cross)
    for plane in range(count - 1, -1, -1):
        step = planes[plane, 3, 1:2]
        jxx, jxy, jyy = planes[plane, 0], planes[plane, 1], planes[plane, 2]
        tb_one = tb_one + step * xb_one
        tb_two = tb_two + step * xb_two
        adjoints[plane, 0] = -tb_one
        adjoints[plane, 1] = -tb_two
        xb_one, xb_two = (
            xb_one - (jxx * tb_one + jxy * tb_two),
            xb_two - (jxy * tb_one + jyy * tb_two),
        )


def per_device(tidal, plane_weight, plane_step, ray_angle, dest_tile, dest_segment, interp):
    n_tile = lax.axis_size("tile")
    n_depth = lax.axis_size("depth")
    rays = tidal.shape[2]
    part = rays // n_depth
    blocks = interp.shape[1]
    width = interp.shape[2]
    slots = 2 * blocks // n_tile
    segments = ROWS * COLS // width
    here = lax.axis_index("depth")
    tile = lax.axis_index("tile")

    lanes = part // width
    row = lax.broadcasted_iota(jnp.int32, (n_depth, 1, lanes, width), 2)
    scalars = jnp.where(row == 0, plane_weight[0], plane_step[0])
    terms = jnp.transpose(tidal[0].reshape(3, n_depth, lanes, width), (1, 0, 2, 3))
    planes = all_to_all(jnp.concatenate([terms, scalars], axis=1), "depth")
    angle = lax.dynamic_slice(ray_angle, (here * part,), (part,)).reshape(lanes, width)
    trig = jnp.stack(
        [jnp.sin(2.0 * angle), jnp.cos(2.0 * angle), jnp.sin(angle), jnp.cos(angle)]
    )
    adjoints = pl.pallas_call(
        sweep_kernel,
        out_shape=jax.ShapeDtypeStruct((n_depth, 2, lanes, width), jnp.float32),
        in_specs=[pl.BlockSpec(memory_space=pltpu.VMEM)] * 2,
        out_specs=pl.BlockSpec(memory_space=pltpu.VMEM),
    )(planes, trig)
    back = lax.reduce_precision(all_to_all(adjoints, "depth"), 8, 7)
    abar = jnp.transpose(back, (0, 2, 1, 3))
    abar = abar.reshape(blocks, 2, width).astype(jnp.bfloat16)
    contrib = jnp.einsum("bcr,brk->bck", abar, interp[0], preferred_element_type=jnp.float32)

    dest = dest_tile[0, :, 0]
    earlier = jnp.arange(blocks)[None, :] < jnp.arange(blocks)[:, None]
    rank = jnp.sum(jnp.logical_and(dest[:, None] == dest[None, :], earlier), axis=1)
    slot = dest * slots + rank
    pick = (jnp.arange(n_tile * slots)[:, None] == slot[None, :]).astype(jnp.float32)
    send_data = jnp.dot(pick, contrib.reshape(blocks, 2 * width), precision=HI)
    send_ids = jnp.dot(pick, (dest_segment[0] + 1).astype(jnp.float32)[:, None], precision=HI) - 1.0
    got_data = all_to_all(send_data.reshape(n_tile, slots, 2 * width), "tile")
    got_ids = all_to_all(send_ids.astype(jnp.int32).reshape(n_tile, slots), "tile")
    place = (jnp.arange(segments)[:, None] == got_ids.reshape(1, -1)).astype(jnp.float32)
    summed = jnp.dot(place, got_data.reshape(-1, 2 * width), precision=HI)
    ax = summed[:, :width].reshape(ROWS, COLS)
    ay = summed[:, width:].reshape(ROWS, COLS)

    left, right = shift_cols(ax)
    column = 0.5 * (left - right)
    above = jnp.where(tile == 0, 0.0, -0.5 * ay[0])
    below = jnp.where(tile == n_tile - 1, 0.0, 0.5 * ay[1])
    raw_0 = column[0] - 0.5 * ay[1]
    raw_1 = column[1] + 0.5 * ay[0]
    up = jnp.stack([0.25 * above, 0.5 * above + 0.25 * raw_0])
    down = jnp.stack([0.25 * raw_1 + 0.5 * below, 0.25 * below])
    own = jnp.stack(
        [0.25 * above + 0.5 * raw_0 + 0.25 * raw_1, 0.25 * raw_0 + 0.5 * raw_1 + 0.25 * below]
    )
    to_next = [(i, i + 1) for i in range(n_tile - 1)]
    from_next = [(j, i) for i, j in to_next]
    rows_done = own + lax.ppermute(down, "tile", to_next) + lax.ppermute(up, "tile", from_next)
    left, right = shift_cols(rows_done)
    return (0.25 * left + 0.5 * rows_done + 0.25 * right)[None]


def solution(mesh):
    return jax.shard_map(
        per_device,
        mesh=mesh,
        in_specs=(
            P("depth", None, "tile"),
            P("depth"),
            P("depth"),
            P("tile"),
            P("depth", "tile", None),
            P("depth", "tile"),
            P("depth", "tile", None, None),
        ),
        out_specs=P("depth", "tile", None),
        check_vma=False,
    )
```

time: 642 us -> 78.7 us (0.12)
  the two profiles are of different devices: /device:TPU:103 before, /device:TPU:1 now
where the time goes in v1:
time: 78.7 us; the launch traced here: 78.1 us
  starting transfers between devices  33.8 us (43%)
  waiting for transfers between devices  25.8 us (33%)
  other arithmetic  6.54 us (8%)
  matrix products  5.47 us (7%)
  local copies, waits for them, and re-layouts  3.22 us (4%)
  Pallas kernels  1.82 us (2%)
  between operations  1.46 us (2%)
    all_to_all x4, starting transfers between devices, all_to_all(): return lax.all_to_all(value, axis, split_axis=0, concat_axis=0, tiled=True)  28.7 us
    all_to_all x4, waiting for transfers between devices, all_to_all(): return lax.all_to_all(value, axis, split_axis=0, concat_axis=0, tiled=True)  21.4 us
    ppermute x1, waiting for transfers between devices, per_device(): lax.ppermute(up, 'tile', from_next)  4.35 us
    dot_general x1, matrix products, per_device(): jnp.einsum('bcr,brk->bck', abar, interp[0], preferred_element_type=jnp.fl...  3.37 us
    ppermute x1, starting transfers between devices, per_device(): lax.ppermute(down, 'tile', to_next)  3.12 us
    ppermute x1, starting transfers between devices, per_device(): lax.ppermute(up, 'tile', from_next)  1.92 us
    pallas_call x1, Pallas kernels, per_device(): pl.pallas_call(sweep_kernel, out_shape=jax.ShapeDtypeStruct((n_depth, 2,...  1.82 us
  transfers between devices with their start and end apart: 6, of which 4 were waited for; matrix products, arithmetic and copies ran while one was open for 12% of the time, Pallas kernels for 0%

profile of v1, /device:TPU:1, one launch (start us, length us, event | category | flops | bytes accessed | tf_op | source)
XLA Modules:
  0.0 78.1 jit_solution(14339428184968273608)
XLA Ops:
  1.3 1.0 %copy.17 = f32[3,32,4,128]{3,2,0,1:T(4,128)S(1)} copy(f32[3,32,4,128]{3,2,1,0:T(4,128)} %bitcast.46) | data formatting | bytes 393216 | tf_op jit(solution)/shard_map/reshape;squeeze | solution.py:61
  2.3 0.1 iota.31
  2.4 0.8 pad_maximum_fusion
  3.1 11.9 %all-to-all-start.1 = ((f32[32,4,4,128]{3,2,1,0:T(4,128)}), f32[32,4,4,128]{3,2,1,0:T(4,128)S(1)}, u32[]{:S(2)}, u32[]{:S(2)}) async-start(f32[32,4,4,128]{3,2,1,0:T(4,128)} %pad_maximum_fusion), calls=%async_computation.1 | async-start | bytes 524288 | tf_op jit(solution)/shard_map/all_to_all | solution.py:14
  15.0 0.9 %convert_reduce_fusion = s32[128]{0:T(128)S(1)} fusion(s32[128]{0:T(128)} %bitcast.48), kind=kLoop, calls=%fused_computation.31 | loop fusion | flops 81792 | bytes 1024 | tf_op jit(solution)/shard_map/reduce_sum | solution.py:80
  15.9 0.8 %sine_bitcast_fusion.1 = (f32[1,4,128]{2,1,0:T(4,128)S(1)}, f32[1,4,128]{2,1,0:T(4,128)S(1)}, f32[1,4,128]{2,1,0:T(4,128)S(1)}, f32[1,4,128]{2,1,0:T(4,128)S(1)}) fusion(f32[16384]{0:T(1024)} %param.10, s32[]{:T(128)S(6)} %select_n.51), kind=kLoop, calls=%fused_computation.44 | loop fusion | flops 512 | bytes 10244 | tf_op jit(solution)/shard_map/sin | solution.py:65
  16.7 0.6 pad_maximum_fusion.3.trig
  17.3 0.7 multiply_add_fusion.3
  17.9 0.8 fusion.7
  18.7 7.5 %all-to-all-done.1.planes = f32[32,4,4,128]{3,2,1,0:T(4,128)S(1)} async-done(((f32[32,4,4,128]{3,2,1,0:T(4,128)}), f32[32,4,4,128]{3,2,1,0:T(4,128)S(1)}, u32[]{:S(2)}, u32[]{:S(2)}) %all-to-all-start.1) | async-done | bytes 262176 | tf_op jit(solution)/shard_map/all_to_all | solution.py:14
  26.3 0.0 copy-start
  26.3 0.7 copy-done
  27.0 1.8 %shard_map.73 = f32[32,2,4,128]{3,2,1,0:T(4,128)} custom-call(f32[32,4,4,128]{3,2,1,0:T(4,128)} %copy-done, f32[4,4,128]{2,1,0:T(4,128)} %pad_maximum_fusion.3.trig), custom_call_target="tpu_custom_call" | custom-call | tf_op jit(solution)/shard_map/pallas_call | solution.py:67
  28.8 4.7 %all-to-all-start.2 = ((f32[32,2,4,128]{3,2,1,0:T(4,128)}), f32[32,2,4,128]{3,2,1,0:T(4,128)S(1)}, u32[]{:S(2)}, u32[]{:S(2)}) async-start(f32[32,2,4,128]{3,2,1,0:T(4,128)} %shard_map.73), calls=%async_computation.2 | async-start | bytes 262144 | tf_op jit(solution)/shard_map/all_to_all | solution.py:14
  33.5 0.7 all_to_all.15
  34.2 8.7 %all-to-all-done.2 = f32[32,2,4,128]{3,2,1,0:T(4,128)S(1)} async-done(((f32[32,2,4,128]{3,2,1,0:T(4,128)}), f32[32,2,4,128]{3,2,1,0:T(4,128)S(1)}, u32[]{:S(2)}, u32[]{:S(2)}) %all-to-all-start.2) | async-done | bytes 131104 | tf_op jit(solution)/shard_map/all_to_all | solution.py:14
  42.8 7.4 %all-to-all-start = ((s32[8,1,32]{2,1,0:T(1,128)}), s32[8,1,32]{2,1,0:T(1,128)S(1)}, u32[]{:S(2)}, u32[]{:S(2)}) async-start(s32[8,1,32]{2,1,0:T(1,128)} %all_to_all.15), calls=%async_computation | async-start | bytes 8192 | tf_op jit(solution)/shard_map/all_to_all | solution.py:14
  50.3 3.4 %fusion = f32[128,2,128]{2,1,0:T(2,128)S(1)} fusion(bf16[1,128,128,128]{3,2,1,0:T(8,128)(2,1)} %param.13, bf16[128,2,128]{2,0,1:T(8,128)(2,1)S(1)} %bitcast.42), kind=kOutput, calls=%fused_computation | convolution fusion | flops 8388608 | bytes 4390912 | tf_op jit(solution)/shard_map/bcr,brk->bck/dot_general | solution.py:76
  53.7 0.1 reshape.192
  53.8 1.0 %fusion.5 = f32[8,32,256]{2,1,0:T(8,128)} fusion(f32[128,256,1]{1,0,2:T(8,128)S(1)} %reshape.192, s32[128]{0:T(128)S(1)} %multiply_add_fusion.3, s32[8,32]{1,0:T(8,128)S(1)} %multiply_add_fusion.2), kind=kOutput, calls=%fused_computation.16 | convolution fusion | flops 100696064 | bytes 394752 | tf_op jit(solution)/shard_map/dot_general | solution.py:83
  54.8 0.0 all-to-all-done
  54.8 4.8 %all-to-all-start.3 = ((f32[8,32,256]{2,1,0:T(8,128)}), f32[8,32,256]{2,1,0:T(8,128)S(1)}, u32[]{:S(2)}, u32[]{:S(2)}) async-start(f32[8,32,256]{2,1,0:T(8,128)} %fusion.5), calls=%async_computation.3 | async-start | bytes 524288 | tf_op jit(solution)/shard_map/all_to_all | solution.py:14
  59.6 0.5 broadcast.241
  60.1 0.7 reduce.3
  60.8 0.1 eq.79
  60.9 5.2 %all-to-all-done.3 = f32[8,32,256]{2,1,0:T(8,128)S(1)} async-done(((f32[8,32,256]{2,1,0:T(8,128)}), f32[8,32,256]{2,1,0:T(8,128)S(1)}, u32[]{:S(2)}, u32[]{:S(2)}) %all-to-all-start.3) | async-done | bytes 262176 | tf_op jit(solution)/shard_map/all_to_all | solution.py:14
  66.1 0.3 fusion.2
  66.4 0.1 reshape.189
  66.5 0.3 subtract_multiply_fusion
  66.9 0.4 add_add_fusion.1
  67.2 0.1 pad_maximum_fusion.2
  67.4 0.1 pad_maximum_fusion.1
  67.5 3.1 %collective-permute-start = (f32[2,16384]{1,0:T(2,128)S(1)}, f32[2,16384]{1,0:T(2,128)S(1)}, u32[]{:S(2)}, u32[]{:S(2)}) collective-permute-start(f32[2,16384]{1,0:T(2,128)S(1)} %pad_maximum_fusion.1), channel_id=1, source_target_pairs={{0,1},{1,2},{2,3},{3,4},{4,5},{5,6},{6,7},{8,9},{9,10},{10,11},{11... | collective-permute-start | bytes 393224 | tf_op jit(solution)/shard_map/ppermute | solution.py:105
  70.6 1.9 %collective-permute-start.1 = (f32[2,16384]{1,0:T(2,128)S(1)}, f32[2,16384]{1,0:T(2,128)S(1)}, u32[]{:S(2)}, u32[]{:S(2)}) collective-permute-start(f32[2,16384]{1,0:T(2,128)S(1)} %pad_maximum_fusion.2), channel_id=1, source_target_pairs={{1,0},{2,1},{3,2},{4,3},{5,4},{6,5},{7,6},{9,8},{10,9},{11,10},{12... | collective-permute-start | bytes 393224 | tf_op jit(solution)/shard_map/ppermute | solution.py:105
  72.5 0.0 collective-permute-done
  72.6 4.3 %collective-permute-done.1 = f32[2,16384]{1,0:T(2,128)S(1)} collective-permute-done((f32[2,16384]{1,0:T(2,128)S(1)}, f32[2,16384]{1,0:T(2,128)S(1)}, u32[]{:S(2)}, u32[]{:S(2)}) %collective-permute-start.1) | collective-permute-done | bytes 131104 | tf_op jit(solution)/shard_map/ppermute | solution.py:105
  76.9 0.2 fusion.3
  77.1 1.0 %add_bitcast_fusion = f32[1,2,16384]{2,1,0:T(2,128)} fusion(f32[2,16384]{1,0:T(2,128)S(1)} %fusion.3), kind=kLoop, calls=%fused_computation.10 | loop fusion | flops 163840 | bytes 262144 | tf_op jit(solution)/shard_map/broadcast_in_dim | solution.py:107
  (7 shorter events, 0.1 us)
Async XLA Ops:
  3.1 23.2 %all-to-all-start.1 = ((f32[32,4,4,128]{3,2,1,0:T(4,128)}), f32[32,4,4,128]{3,2,1,0:T(4,128)S(1)}, u32[]{:S(2)}, u32[]{:S(2)}) async-start(f32[32,4,4,128]{3,2,1,0:T(4,128)} %pad_maximum_fusion), calls=%async_computation.1 | async-start | bytes 524288 | tf_op jit(solution)/shard_map/all_to_all | solution.py:14
  26.3 0.7 copy-start
  28.8 14.1 %all-to-all-start.2 = ((f32[32,2,4,128]{3,2,1,0:T(4,128)}), f32[32,2,4,128]{3,2,1,0:T(4,128)S(1)}, u32[]{:S(2)}, u32[]{:S(2)}) async-start(f32[32,2,4,128]{3,2,1,0:T(4,128)} %shard_map.73), calls=%async_computation.2 | async-start | bytes 262144 | tf_op jit(solution)/shard_map/all_to_all | solution.py:14
  42.8 12.0 %all-to-all-start = ((s32[8,1,32]{2,1,0:T(1,128)}), s32[8,1,32]{2,1,0:T(1,128)S(1)}, u32[]{:S(2)}, u32[]{:S(2)}) async-start(s32[8,1,32]{2,1,0:T(1,128)} %all_to_all.15), calls=%async_computation | async-start | bytes 8192 | tf_op jit(solution)/shard_map/all_to_all | solution.py:14
  54.8 11.3 %all-to-all-start.3 = ((f32[8,32,256]{2,1,0:T(8,128)}), f32[8,32,256]{2,1,0:T(8,128)S(1)}, u32[]{:S(2)}, u32[]{:S(2)}) async-start(f32[8,32,256]{2,1,0:T(8,128)} %fusion.5), calls=%async_computation.3 | async-start | bytes 524288 | tf_op jit(solution)/shard_map/all_to_all | solution.py:14
  67.5 5.1 %collective-permute-start = (f32[2,16384]{1,0:T(2,128)S(1)}, f32[2,16384]{1,0:T(2,128)S(1)}, u32[]{:S(2)}, u32[]{:S(2)}) collective-permute-start(f32[2,16384]{1,0:T(2,128)S(1)} %pad_maximum_fusion.1), channel_id=1, source_target_pairs={{0,1},{1,2},{2,3},{3,4},{4,5},{5,6},{6,7},{8,9},{9,10},{10,11},{11... | collective-permute-start | bytes 393224 | tf_op jit(solution)/shard_map/ppermute | solution.py:105
  70.6 6.3 %collective-permute-start.1 = (f32[2,16384]{1,0:T(2,128)S(1)}, f32[2,16384]{1,0:T(2,128)S(1)}, u32[]{:S(2)}, u32[]{:S(2)}) collective-permute-start(f32[2,16384]{1,0:T(2,128)S(1)} %pad_maximum_fusion.2), channel_id=1, source_target_pairs={{1,0},{2,1},{3,2},{4,3},{5,4},{6,5},{7,6},{9,8},{10,9},{11,10},{12... | collective-permute-start | bytes 393224 | tf_op jit(solution)/shard_map/ppermute | solution.py:105

commit v2 on v1

v2 whole, which is shorter than its diff:
```python
import jax
import jax.numpy as jnp
from jax import lax
from jax.experimental import pallas as pl
from jax.experimental.pallas import tpu as pltpu
from jax.sharding import PartitionSpec as P

ROWS = 2
WIDTH = 128
X_SIZE = 4
MESH = pl.DeviceIdType.MESH
F32 = jnp.float32
BF16 = jnp.bfloat16


def split_two(value):
    high = value.astype(BF16)
    low = (value - high.astype(F32)).astype(BF16)
    return jnp.concatenate([high, low], axis=1)


def iota(shape, axis):
    return lax.broadcasted_iota(jnp.int32, shape, axis)


def neighbours(field):
    lane, row = iota(field.shape, 1), iota(field.shape, 0)
    rows, lanes = field.shape
    left = pltpu.roll(field, 1, axis=1)
    left = jnp.where(lane == 0, pltpu.roll(left, 1, axis=0), left)
    left = jnp.where(jnp.logical_and(lane == 0, row == 0), 0.0, left)
    right = pltpu.roll(field, lanes - 1, axis=1)
    right = jnp.where(lane == lanes - 1, pltpu.roll(right, rows - 1, axis=0), right)
    right = jnp.where(jnp.logical_and(lane == lanes - 1, row == rows - 1), 0.0, right)
    return left, right


def kernel(
    n_depth, n_tile,
    tidal, angle, interp, dest, segment, weight, step,
    out,
    tid, ang, itp, dst, seg, mine, scalars, planes, adj, back, contrib, pick,
    id_send, id_got, send, got, place, up, down, from_above, from_below,
    local_sem, send_sem, recv_sem,
):
    depth, tile = lax.axis_index("depth"), lax.axis_index("tile")
    blocks = interp.shape[0]
    lanes = blocks // n_depth
    slots = 2 * blocks // n_tile
    columns = 2 * blocks
    segments = place.shape[0]
    rows = segments // ROWS
    n_z, n_x = n_depth // X_SIZE, X_SIZE
    z, x = depth // n_x, depth % n_x
    z_order = sorted(range(n_z), key=lambda dz: -min(dz, n_z - dz))
    x_order = sorted(range(n_x), key=lambda dx: -min(dx, n_x - dx))
    depth_peers = [
        lax.rem(z + dz, n_z) * n_x + lax.rem(x + dx, n_x)
        for dz in z_order for dx in x_order if dz or dx
    ]
    tile_peers = [lax.rem(tile + dt, n_tile) for dt in (3, 5, 4, 2, 6, 1, 7) if dt < n_tile]

    barrier = pltpu.get_barrier_semaphore()
    for peer in depth_peers:
        pl.semaphore_signal(barrier, 1, device_id=(peer, tile), device_id_type=MESH)
    for peer in tile_peers:
        pl.semaphore_signal(barrier, 1, device_id=(depth, peer), device_id_type=MESH)

    loads = [
        pltpu.make_async_copy(source, target, local_sem.at[i])
        for i, (source, target) in enumerate(
            [(tidal, tid), (dest, dst), (segment, seg), (angle, ang), (interp, itp)]
        )
    ]
    for load in loads:
        load.start()
    mine[...] = jnp.where(iota(mine.shape, 0) == 0, weight[0], step[0])
    scalars[depth] = mine[...]
    for load in loads[1:3]:
        load.wait()

    dest_row = jnp.broadcast_to(dst[...], (blocks, blocks)).astype(F32)
    dest_column = dest_row.T
    below_diagonal = iota((blocks, blocks), 0) > iota((blocks, blocks), 1)
    same = (dest_row == dest_column).astype(F32)
    rank_column = jnp.sum(jnp.where(below_diagonal, same, 0.0), axis=1, keepdims=True)
    rank_row = jnp.sum(
        jnp.where(iota((blocks, blocks), 0) < iota((blocks, blocks), 1), same, 0.0),
        axis=0, keepdims=True,
    )
    owner = iota((n_tile, blocks), 0).astype(F32)
    ids = jnp.where(
        jnp.broadcast_to(dst[...], (n_tile, blocks)).astype(F32) == owner,
        jnp.broadcast_to(seg[...], (n_tile, blocks)).astype(F32) + 1.0, 0.0,
    ).astype(BF16)
    at = (rank_column + (tile * slots).astype(F32) == iota((blocks, columns), 1).astype(F32))
    id_rows = jnp.dot(ids, at.astype(F32).astype(BF16), preferred_element_type=F32)
    for t in range(n_tile):
        for h in range(2):
            id_send[t, h:h + 1, :] = id_rows[t:t + 1, h * blocks:(h + 1) * blocks]
    id_got[tile] = id_send[tile]

    slot_row = (dest_row[0:8] * float(slots) + rank_row).astype(BF16)
    q = iota((blocks, columns), 1)
    spread = (iota((blocks, columns), 0) == (q // (2 * lanes)) * lanes + q % lanes)
    slot_q = jnp.dot(slot_row, spread.astype(F32).astype(BF16), preferred_element_type=F32)[0:1]
    q = iota((1, columns), 1)
    key_q = slot_q + ((q // lanes) % 2 * 1024).astype(F32)
    row = iota((2 * n_tile * slots, columns), 0)
    key_row = (row // (2 * slots)) * slots + row % slots + (row // slots) % 2 * 1024
    pick[...] = (key_row.astype(F32) == key_q).astype(F32).astype(BF16)

    loads[0].wait()
    loads[3].wait()
    planes[depth] = tid[:, depth]
    a = ang[depth]
    sin_a, cos_a = jnp.sin(a), jnp.cos(a)
    sin_2a, cos_2a = jnp.sin(2.0 * a), jnp.cos(2.0 * a)

    pl.semaphore_wait(barrier, len(depth_peers) + len(tile_peers))

    def push(source, target, kind, where):
        copy = pltpu.make_async_remote_copy(
            src_ref=source, dst_ref=target, send_sem=send_sem.at[kind], recv_sem=recv_sem.at[kind],
            device_id=where, device_id_type=MESH,
        )
        copy.start()

    def settle(ref, sem):
        pltpu.make_async_copy(ref, ref, sem).wait()

    for peer in depth_peers:
        push(mine, scalars.at[depth], 0, (peer, tile))
        push(tid.at[:, peer], planes.at[depth], 1, (peer, tile))
    for peer in tile_peers:
        push(id_send.at[peer], id_got.at[tile], 2, (depth, peer))

    n_other = n_depth - 1
    settle(scalars.at[pl.ds(0, n_other)], recv_sem.at[0])
    settle(planes.at[pl.ds(0, n_other)], recv_sem.at[1])
    g_one = jnp.zeros((lanes, WIDTH), F32)
    g_two = jnp.zeros((lanes, WIDTH), F32)
    for plane in range(n_depth):
        w = scalars[plane, 0:1]
        g_one -= w * (planes[plane, 0] - planes[plane, 2]) * 0.5
        g_two -= w * planes[plane, 1]
    cross = -g_one * sin_2a + g_two * cos_2a
    xb_one, xb_two = cross * cos_a, cross * sin_a
    tb_one = tb_two = jnp.zeros_like(cross)
    for plane in range(n_depth - 1, -1, -1):
        s = scalars[plane, 1:2]
        jxx, jxy, jyy = planes[plane, 0], planes[plane, 1], planes[plane, 2]
        tb_one = tb_one + s * xb_one
        tb_two = tb_two + s * xb_two
        adj[plane, 0:lanes] = -tb_one
        adj[plane, lanes:2 * lanes] = -tb_two
        xb_one, xb_two = (
            xb_one - (jxx * tb_one + jxy * tb_two),
            xb_two - (jxy * tb_one + jyy * tb_two),
        )
    for peer in depth_peers:
        push(adj.at[peer], back.at[depth], 3, (peer, tile))
    back[depth] = adj[depth]

    settle(id_got.at[pl.ds(0, n_tile - 1)], recv_sem.at[2])
    id_sum = jnp.sum(id_got[...], axis=0) - 1.0
    seg_row = iota((segments, blocks), 0).astype(F32)
    for h in range(2):
        place[:, h * blocks:(h + 1) * blocks] = (
            (seg_row == id_sum[h:h + 1]).astype(F32).astype(BF16)
        )
    loads[4].wait()
    settle(back.at[pl.ds(0, n_other)], recv_sem.at[3])
    part = iota((2 * lanes, WIDTH), 0) % lanes
    for i in range(n_depth):
        value = back[i]
        left = jnp.concatenate([jnp.where(part == j, value, 0.0) for j in range(lanes)], axis=1)
        contrib[2 * lanes * i:2 * lanes * (i + 1), :] = jnp.dot(
            left.astype(BF16), itp[lanes * i:lanes * (i + 1)].reshape(lanes * WIDTH, WIDTH),
            preferred_element_type=F32,
        )
    picked = jnp.dot(pick[...], split_two(contrib[...]), preferred_element_type=F32)
    picked = picked[:, 0:WIDTH] + picked[:, WIDTH:2 * WIDTH]
    send[...] = picked.reshape(send.shape)
    for peer in tile_peers:
        push(send.at[peer], got.at[tile], 4, (depth, peer))
    got[tile] = send[tile]
    settle(got.at[pl.ds(0, n_tile - 1)], recv_sem.at[4])

    both = [
        split_two(got[:, c * slots:(c + 1) * slots, :].reshape(n_tile * slots, WIDTH))
        for c in range(2)
    ]
    ax, ay = [
        total[:, 0:WIDTH] + total[:, WIDTH:2 * WIDTH]
        for total in (jnp.dot(place[...], b, preferred_element_type=F32) for b in both)
    ]
    ay_0, ay_1 = ay[0:rows], ay[rows:]
    above = jnp.where(tile == 0, 0.0, -0.5) * ay_0
    below = jnp.where(tile == n_tile - 1, 0.0, 0.5) * ay_1
    left, right = neighbours(ax[0:rows])
    raw_0 = 0.5 * (left - right) - 0.5 * ay_1
    left, right = neighbours(ax[rows:])
    raw_1 = 0.5 * (left - right) + 0.5 * ay_0
    up[0] = 0.25 * above
    up[1] = 0.5 * above + 0.25 * raw_0
    down[0] = 0.25 * raw_1 + 0.5 * below
    down[1] = 0.25 * below
    before, after = lax.rem(tile + n_tile - 1, n_tile), lax.rem(tile + 1, n_tile)
    push(up, from_below, 5, (depth, before))
    push(down, from_above, 6, (depth, after))
    own = [
        0.25 * above + 0.5 * raw_0 + 0.25 * raw_1,
        0.25 * raw_0 + 0.5 * raw_1 + 0.25 * below,
    ]
    settle(from_below, recv_sem.at[5])
    settle(from_above, recv_sem.at[6])
    has_before = jnp.where(tile == 0, 0.0, 1.0)
    has_after = jnp.where(tile == n_tile - 1, 0.0, 1.0)
    for r in range(ROWS):
        line = own[r] + has_before * from_above[r] + has_after * from_below[r]
        left, right = neighbours(line)
        out[r] = 0.25 * left + 0.5 * line + 0.25 * right

    settle(scalars.at[pl.ds(0, n_other)], send_sem.at[0])
    settle(planes.at[pl.ds(0, n_other)], send_sem.at[1])
    settle(id_got.at[pl.ds(0, n_tile - 1)], send_sem.at[2])
    settle(back.at[pl.ds(0, n_other)], send_sem.at[3])
    settle(got.at[pl.ds(0, n_tile - 1)], send_sem.at[4])
    settle(up, send_sem.at[5])
    settle(down, send_sem.at[6])


def per_device(tidal, plane_weight, plane_step, ray_angle, dest_tile, dest_segment, interp):
    n_tile = lax.axis_size("tile")
    n_depth = lax.axis_size("depth")
    rays = tidal.shape[2]
    blocks = interp.shape[1]
    lanes = blocks // n_depth
    slots = 2 * blocks // n_tile
    segments = 2 * blocks
    rows = segments // ROWS

    def body(*refs):
        kernel(n_depth, n_tile, *refs)

    hbm = pl.BlockSpec(memory_space=pl.ANY)
    smem = pl.BlockSpec(memory_space=pltpu.SMEM)
    vmem = pltpu.VMEM
    out = pl.pallas_call(
        body,
        out_shape=jax.ShapeDtypeStruct((ROWS, rows, WIDTH), F32),
        in_specs=[hbm, hbm, hbm, hbm, hbm, smem, smem],
        out_specs=pl.BlockSpec(memory_space=pltpu.VMEM),
        scratch_shapes=[
            vmem((3, n_depth, lanes, WIDTH), F32),
            vmem((n_depth, lanes, WIDTH), F32),
            vmem((blocks, WIDTH, WIDTH), BF16),
            vmem((1, blocks), jnp.int32),
            vmem((1, blocks), jnp.int32),
            vmem((2, WIDTH), F32),
            vmem((n_depth, 2, WIDTH), F32),
            vmem((n_depth, 3, lanes, WIDTH), F32),
            vmem((n_depth, 2 * lanes, WIDTH), F32),
            vmem((n_depth, 2 * lanes, WIDTH), F32),
            vmem((2 * blocks, WIDTH), F32),
            vmem((2 * n_tile * slots, 2 * blocks), BF16),
            vmem((n_tile, 2, blocks), F32),
            vmem((n_tile, 2, blocks), F32),
            vmem((n_tile, 2 * slots, WIDTH), F32),
            vmem((n_tile, 2 * slots, WIDTH), F32),
            vmem((segments, 2 * blocks), BF16),
            vmem((ROWS, rows, WIDTH), F32),
            vmem((ROWS, rows, WIDTH), F32),
            vmem((ROWS, rows, WIDTH), F32),
            vmem((ROWS, rows, WIDTH), F32),
            pltpu.SemaphoreType.DMA((5,)),
            pltpu.SemaphoreType.DMA((7,)),
            pltpu.SemaphoreType.DMA((7,)),
        ],
        compiler_params=pltpu.CompilerParams(collective_id=0, has_side_effects=True),
    )(
        tidal.reshape(3, n_depth, lanes, WIDTH),
        ray_angle.reshape(n_depth, lanes, WIDTH),
        interp[0],
        dest_tile.reshape(1, blocks),
        dest_segment,
        plane_weight,
        plane_step,
    )
    return out.reshape(1, ROWS, rows * WIDTH)


def solution(mesh):
    return jax.shard_map(
        per_device,
        mesh=mesh,
        in_specs=(
            P("depth", None, "tile"),
            P("depth"),
            P("depth"),
            P("tile"),
            P("depth", "tile", None),
            P("depth", "tile"),
            P("depth", "tile", None, None),
        ),
        out_specs=P("depth", "tile", None),
        check_vma=False,
    )
```

time: 78.7 us -> 38.9 us (0.49)
  Pallas kernels: 1.82 us -> 35.9 us
  starting transfers between devices: 33.8 us -> 0 us
  waiting for transfers between devices: 25.8 us -> 0 us
  other arithmetic: 6.54 us -> 0 us
  matrix products: 5.47 us -> 0 us
  local copies, waits for them, and re-layouts: 3.22 us -> 1.64 us
    pallas_call x1, Pallas kernels: 1.82 us -> 35.9 us  [per_device(): pl.pallas_call(body, out_shape=jax.ShapeDtypeStruct((ROWS, rows, WIDTH),...]
    all_to_all x4 -> x0, starting transfers between devices: 28.7 us -> none  [all_to_all(): return lax.all_to_all(value, axis, split_axis=0, concat_axis=0, tiled=True)]
    all_to_all x4 -> x0, waiting for transfers between devices: 21.4 us -> none  [all_to_all(): return lax.all_to_all(value, axis, split_axis=0, concat_axis=0, tiled=True)]
    dot_general x4 -> x0, matrix products: 5.47 us -> none  [the longest x1 3.37 us: per_device(): jnp.einsum('bcr,brk->bck', abar, interp[0], preferred_element_type=jnp.fl...]
    ppermute x2 -> x0, starting transfers between devices: 5.04 us -> none  [the longest x1 3.12 us: per_device(): lax.ppermute(down, 'tile', to_next)]
    ppermute x2 -> x0, waiting for transfers between devices: 4.35 us -> none  [the longest x1 4.35 us: per_device(): lax.ppermute(up, 'tile', from_next)]
    reshape x2 -> x1, local copies, waits for them, and re-layouts: 0.19 us -> 1.64 us  [per_device(): return out.reshape(1, ROWS, rows * WIDTH)]
    all_to_all x2 -> x0, local copies, waits for them, and re-layouts: 1.18 us -> none  [all_to_all(): return lax.all_to_all(value, axis, split_axis=0, concat_axis=0, tiled=True)]
  transfers between devices with their start and end apart: 6 -> 0, of which waited for: 4 -> 0; matrix products, arithmetic and copies ran while one was open for 12% -> 0% of each run, Pallas kernels for 0% -> 0%
where the time goes in v2:
time: 38.9 us; the launch traced here: 38.8 us
  Pallas kernels  35.9 us (92%)
  local copies, waits for them, and re-layouts  1.64 us (4%)
  between operations  1.3 us (3%)
    pallas_call x1, Pallas kernels, per_device(): pl.pallas_call(body, out_shape=jax.ShapeDtypeStruct((ROWS, rows, WIDTH),...  35.9 us
    reshape x1, local copies, waits for them, and re-layouts, per_device(): return out.reshape(1, ROWS, rows * WIDTH)  1.64 us

profile of v2, /device:TPU:1, one launch (start us, length us, event | category | flops | bytes accessed | tf_op | source)
XLA Modules:
  0.0 38.8 jit_solution(15706893601973607626)
XLA Ops:
  1.3 35.9 %shard_map.73 = f32[2,128,128]{2,1,0:T(8,128)} custom-call(f32[3,32,4,128]{3,2,1,0:T(4,128)} %bitcast.5, f32[32,4,128]{2,1,0:T(4,128)} %bitcast.6, bf16[128,128,128]{2,1,0:T(8,128)(2,1)} %bitcast.4, s32[1,128]{1,0:T(1,128)} %bitcast.7, s32[1,128]{1,0:T(1,128)} %refs_4_.1, f32[1]{0:T(128)S(6)} %copy.8.refs_5_, f32[1]{0:T(128)S(6)} %copy.9.refs_6_), custom_call_target="tpu_custom_call" | custom-call | tf_op jit(solution)/shard_map/pallas_call | solution.py:250
  37.2 1.6 %reshape.15 = f32[1,2,16384]{2,1,0:T(2,128)} reshape(f32[2,128,128]{2,1,0:T(8,128)} %shard_map.73) | data formatting | bytes 262144 | tf_op jit(solution)/shard_map/reshape | solution.py:291

commit v3 on v2

--- a/solution.py
+++ b/solution.py
@@ -41,7 +41,7 @@
     out,
     tid, ang, itp, dst, seg, mine, scalars, planes, adj, back, contrib, pick,
     id_send, id_got, send, got, place, up, down, from_above, from_below,
-    local_sem, send_sem, recv_sem,
+    local_sem, send_sem, recv_sem, back_sem,
 ):
     depth, tile = lax.axis_index("depth"), lax.axis_index("tile")
     blocks = interp.shape[0]
@@ -58,7 +58,8 @@
         lax.rem(z + dz, n_z) * n_x + lax.rem(x + dx, n_x)
         for dz in z_order for dx in x_order if dz or dx
     ]
-    tile_peers = [lax.rem(tile + dt, n_tile) for dt in (3, 5, 4, 2, 6, 1, 7) if dt < n_tile]
+    far_first = sorted(range(n_tile), key=lambda dt: -min(dt, n_tile - dt))
+    tile_peers = [lax.rem(tile + dt, n_tile) for dt in far_first[:-1]]
 
     barrier = pltpu.get_barrier_semaphore()
     for peer in depth_peers:
@@ -74,10 +75,10 @@
     ]
     for load in loads:
         load.start()
-    mine[...] = jnp.where(iota(mine.shape, 0) == 0, weight[0], step[0])
-    scalars[depth] = mine[...]
     for load in loads[1:3]:
         load.wait()
+    mine[...] = jnp.where(iota(mine.shape, 1) < WIDTH // 2, weight[0], step[0])
+    scalars[depth] = mine[...]
 
     dest_row = jnp.broadcast_to(dst[...], (blocks, blocks)).astype(F32)
     dest_column = dest_row.T
@@ -106,8 +107,11 @@
     slot_q = jnp.dot(slot_row, spread.astype(F32).astype(BF16), preferred_element_type=F32)[0:1]
     q = iota((1, columns), 1)
     key_q = slot_q + ((q // lanes) % 2 * 1024).astype(F32)
-    row = iota((2 * n_tile * slots, columns), 0)
-    key_row = (row // (2 * slots)) * slots + row % slots + (row // slots) % 2 * 1024
+    row = iota((2 * n_tile * slots, 1), 0)
+    turn = row // (2 * slots)
+    owner_row = tile + sum(jnp.where(turn == k, dt, 0) for k, dt in enumerate(far_first))
+    owner_row = jnp.where(owner_row >= n_tile, owner_row - n_tile, owner_row)
+    key_row = owner_row * slots + row % slots + (row // slots) % 2 * 1024
     pick[...] = (key_row.astype(F32) == key_q).astype(F32).astype(BF16)
 
     loads[0].wait()
@@ -141,14 +145,14 @@
     g_one = jnp.zeros((lanes, WIDTH), F32)
     g_two = jnp.zeros((lanes, WIDTH), F32)
     for plane in range(n_depth):
-        w = scalars[plane, 0:1]
+        w = jnp.broadcast_to(scalars[plane, :, 0:1], (lanes, WIDTH))
         g_one -= w * (planes[plane, 0] - planes[plane, 2]) * 0.5
         g_two -= w * planes[plane, 1]
     cross = -g_one * sin_2a + g_two * cos_2a
     xb_one, xb_two = cross * cos_a, cross * sin_a
     tb_one = tb_two = jnp.zeros_like(cross)
     for plane in range(n_depth - 1, -1, -1):
-        s = scalars[plane, 1:2]
+        s = jnp.broadcast_to(scalars[plane, :, WIDTH // 2:WIDTH // 2 + 1], (lanes, WIDTH))
         jxx, jxy, jyy = planes[plane, 0], planes[plane, 1], planes[plane, 2]
         tb_one = tb_one + s * xb_one
         tb_two = tb_two + s * xb_two
@@ -158,8 +162,17 @@
             xb_one - (jxx * tb_one + jxy * tb_two),
             xb_two - (jxy * tb_one + jyy * tb_two),
         )
-    for peer in depth_peers:
-        push(adj.at[peer], back.at[depth], 3, (peer, tile))
+    for peer, dz, dx in [
+        (zt * n_x + lax.rem(x + dx, n_x), zt, dx) for zt in (0, 1, 7, 2, 6, 3, 5, 4) for dx in x_order
+    ]:
+        copy = pltpu.make_async_remote_copy(
+            src_ref=adj.at[peer], dst_ref=back.at[depth], send_sem=send_sem.at[3],
+            recv_sem=back_sem.at[z], device_id=(peer, tile), device_id_type=MESH,
+        )
+        if dx:
+            copy.start()
+        else:
+            pl.when(peer != depth)(copy.start)
     back[depth] = adj[depth]
 
     settle(id_got.at[pl.ds(0, n_tile - 1)], recv_sem.at[2])
@@ -170,21 +183,34 @@
             (seg_row == id_sum[h:h + 1]).astype(F32).astype(BF16)
         )
     loads[4].wait()
-    settle(back.at[pl.ds(0, n_other)], recv_sem.at[3])
     part = iota((2 * lanes, WIDTH), 0) % lanes
-    for i in range(n_depth):
-        value = back[i]
-        left = jnp.concatenate([jnp.where(part == j, value, 0.0) for j in range(lanes)], axis=1)
-        contrib[2 * lanes * i:2 * lanes * (i + 1), :] = jnp.dot(
-            left.astype(BF16), itp[lanes * i:lanes * (i + 1)].reshape(lanes * WIDTH, WIDTH),
+    for dz in sorted(range(n_z), key=lambda dz: min(dz, n_z - dz)):
+        first = lax.rem(z + dz, n_z) * n_x
+        settle(back.at[pl.ds(0, n_x if dz else n_x - 1)], back_sem.at[lax.rem(z + dz, n_z)])
+        for dx in range(n_x):
+            i = first + dx
+            value = back[i]
+            left = jnp.concatenate(
+                [jnp.where(part == j, value, 0.0) for j in range(lanes)], axis=1
+            )
+            at_row = pl.multiple_of(2 * lanes * i, 2 * lanes)
+            contrib[pl.ds(at_row, 2 * lanes), :] = jnp.dot(
+                left.astype(BF16),
+                itp[pl.ds(lanes * i, lanes)].reshape(lanes * WIDTH, WIDTH),
+                preferred_element_type=F32,
+            )
+    source = split_two(contrib[...])
+    half = n_tile // 2
+    for h in range(2):
+        picked = jnp.dot(
+            pick[h * half * 2 * slots:(h + 1) * half * 2 * slots, :], source,
             preferred_element_type=F32,
         )
-    picked = jnp.dot(pick[...], split_two(contrib[...]), preferred_element_type=F32)
-    picked = picked[:, 0:WIDTH] + picked[:, WIDTH:2 * WIDTH]
-    send[...] = picked.reshape(send.shape)
-    for peer in tile_peers:
-        push(send.at[peer], got.at[tile], 4, (depth, peer))
-    got[tile] = send[tile]
+        picked = picked[:, 0:WIDTH] + picked[:, WIDTH:2 * WIDTH]
+        send[h * half:(h + 1) * half] = picked.reshape(half, 2 * slots, WIDTH)
+        for k in range(h * half, min((h + 1) * half, n_tile - 1)):
+            push(send.at[k], got.at[tile], 4, (depth, tile_peers[k]))
+    got[tile] = send[n_tile - 1]
     settle(got.at[pl.ds(0, n_tile - 1)], recv_sem.at[4])
 
     both = [
@@ -198,16 +224,16 @@
     ay_0, ay_1 = ay[0:rows], ay[rows:]
     above = jnp.where(tile == 0, 0.0, -0.5) * ay_0
     below = jnp.where(tile == n_tile - 1, 0.0, 0.5) * ay_1
+    before, after = lax.rem(tile + n_tile - 1, n_tile), lax.rem(tile + 1, n_tile)
     left, right = neighbours(ax[0:rows])
     raw_0 = 0.5 * (left - right) - 0.5 * ay_1
+    up[0] = 0.25 * above
+    up[1] = 0.5 * above + 0.25 * raw_0
+    push(up, from_below, 5, (depth, before))
     left, right = neighbours(ax[rows:])
     raw_1 = 0.5 * (left - right) + 0.5 * ay_0
-    up[0] = 0.25 * above
-    up[1] = 0.5 * above + 0.25 * raw_0
     down[0] = 0.25 * raw_1 + 0.5 * below
     down[1] = 0.25 * below
-    before, after = lax.rem(tile + n_tile - 1, n_tile), lax.rem(tile + 1, n_tile)
-    push(up, from_below, 5, (depth, before))
     push(down, from_above, 6, (depth, after))
     own = [
         0.25 * above + 0.5 * raw_0 + 0.25 * raw_1,
@@ -220,7 +246,7 @@
     for r in range(ROWS):
         line = own[r] + has_before * from_above[r] + has_after * from_below[r]
         left, right = neighbours(line)
-        out[r] = 0.25 * left + 0.5 * line + 0.25 * right
+        out[:, r, :] = 0.25 * left + 0.5 * line + 0.25 * right
 
     settle(scalars.at[pl.ds(0, n_other)], send_sem.at[0])
     settle(planes.at[pl.ds(0, n_other)], send_sem.at[1])
@@ -238,7 +264,7 @@
     blocks = interp.shape[1]
     lanes = blocks // n_depth
     slots = 2 * blocks // n_tile
-    segments = 2 * blocks
+    segments = ROWS * rays // WIDTH
     rows = segments // ROWS
 
     def body(*refs):
@@ -249,7 +275,7 @@
     vmem = pltpu.VMEM
     out = pl.pallas_call(
         body,
-        out_shape=jax.ShapeDtypeStruct((ROWS, rows, WIDTH), F32),
+        out_shape=jax.ShapeDtypeStruct((rows, ROWS, WIDTH), F32),
         in_specs=[hbm, hbm, hbm, hbm, hbm, smem, smem],
         out_specs=pl.BlockSpec(memory_space=pltpu.VMEM),
         scratch_shapes=[
@@ -258,8 +284,8 @@
             vmem((blocks, WIDTH, WIDTH), BF16),
             vmem((1, blocks), jnp.int32),
             vmem((1, blocks), jnp.int32),
-            vmem((2, WIDTH), F32),
-            vmem((n_depth, 2, WIDTH), F32),
+            vmem((1, WIDTH), F32),
+            vmem((n_depth, 1, WIDTH), F32),
             vmem((n_depth, 3, lanes, WIDTH), F32),
             vmem((n_depth, 2 * lanes, WIDTH), F32),
             vmem((n_depth, 2 * lanes, WIDTH), F32),
@@ -277,18 +303,19 @@
             pltpu.SemaphoreType.DMA((5,)),
             pltpu.SemaphoreType.DMA((7,)),
             pltpu.SemaphoreType.DMA((7,)),
+            pltpu.SemaphoreType.DMA((n_depth // X_SIZE,)),
         ],
-        compiler_params=pltpu.CompilerParams(collective_id=0, has_side_effects=True),
+        compiler_params=pltpu.CompilerParams(collective_id=0, vmem_limit_bytes=33554432, has_side_effects=True),
     )(
-        tidal.reshape(3, n_depth, lanes, WIDTH),
-        ray_angle.reshape(n_depth, lanes, WIDTH),
-        interp[0],
-        dest_tile.reshape(1, blocks),
-        dest_segment,
+        pltpu.with_memory_space_constraint(tidal.reshape(3, n_depth, lanes, WIDTH), pltpu.HBM),
+        pltpu.with_memory_space_constraint(ray_angle.reshape(n_depth, lanes, WIDTH), pltpu.HBM),
+        pltpu.with_memory_space_constraint(interp[0], pltpu.HBM),
+        pltpu.with_memory_space_constraint(dest_tile.reshape(1, blocks), pltpu.HBM),
+        pltpu.with_memory_space_constraint(dest_segment, pltpu.HBM),
         plane_weight,
         plane_step,
     )
-    return out.reshape(1, ROWS, rows * WIDTH)
+    return out.transpose(1, 0, 2).reshape(1, ROWS, rows * WIDTH)
 
 
 def solution(mesh):

time: 38.9 us -> 36.3 us (0.933)
  Pallas kernels: 35.9 us -> 34.3 us
  local copies, waits for them, and re-layouts: 1.64 us -> 0.66 us
    reshape x1 -> x0, local copies, waits for them, and re-layouts: 1.64 us -> none  [per_device(): return out.reshape(1, ROWS, rows * WIDTH)]
    pallas_call x1, Pallas kernels: 35.9 us -> 34.3 us  [per_device(): pl.pallas_call(body, out_shape=jax.ShapeDtypeStruct((rows, ROWS, WIDTH),...]
    unnamed x0 -> x1, local copies, waits for them, and re-layouts: none -> 0.66 us
where the time goes in v3:
time: 36.3 us; the launch traced here: 36.2 us
  Pallas kernels  34.3 us (94%)
  between operations  1.3 us (4%)
  local copies, waits for them, and re-layouts  0.66 us (2%)
    pallas_call x1, Pallas kernels, per_device(): pl.pallas_call(body, out_shape=jax.ShapeDtypeStruct((rows, ROWS, WIDTH),...  34.3 us

profile of v3, /device:TPU:1, one launch (start us, length us, event | category | flops | bytes accessed | tf_op | source)
XLA Modules:
  0.0 36.2 jit_solution(17719495539130958091)
XLA Ops:
  1.3 34.3 %shard_map.73 = f32[128,2,128]{2,1,0:T(2,128)S(1)} custom-call(f32[3,32,4,128]{3,2,1,0:T(4,128)} %bitcast.9, f32[32,4,128]{2,1,0:T(4,128)} %bitcast.10, bf16[128,128,128]{2,1,0:T(8,128)(2,1)} %bitcast.8, s32[1,128]{1,0:T(1,128)} %bitcast.11, s32[1,128]{1,0:T(1,128)} %refs_4_.1, f32[1]{0:T(128)S(6)} %copy.9.refs_5_, f32[1]{0:T(128)S(6)} %copy.10.refs_6_), custom_call_target="tpu_custom_call" | custom-call | tf_op jit(solution)/shard_map/pallas_call | solution.py:276
  35.6 0.7 %copy.11 = f32[1,2,16384]{2,1,0:T(2,128)} copy(f32[1,2,16384]{2,1,0:T(2,128)S(1)} %bitcast.7) | data formatting | bytes 262144

commit v4 on v3

--- a/solution.py
+++ b/solution.py
@@ -33,6 +33,11 @@
     right = jnp.where(lane == lanes - 1, pltpu.roll(right, rows - 1, axis=0), right)
     right = jnp.where(jnp.logical_and(lane == lanes - 1, row == rows - 1), 0.0, right)
     return left, right
+
+
+def smooth(line):
+    left, right = neighbours(line)
+    return 0.25 * left + 0.5 * line + 0.25 * right
 
 
 def kernel(
@@ -108,10 +113,11 @@
     q = iota((1, columns), 1)
     key_q = slot_q + ((q // lanes) % 2 * 1024).astype(F32)
     row = iota((2 * n_tile * slots, 1), 0)
-    turn = row // (2 * slots)
+    turn = row // slots % n_tile
     owner_row = tile + sum(jnp.where(turn == k, dt, 0) for k, dt in enumerate(far_first))
     owner_row = jnp.where(owner_row >= n_tile, owner_row - n_tile, owner_row)
-    key_row = owner_row * slots + row % slots + (row // slots) % 2 * 1024
+    y_first = jnp.where(row < n_tile * slots, 1024, 0)
+    key_row = owner_row * slots + row % slots + y_first
     pick[...] = (key_row.astype(F32) == key_q).astype(F32).astype(BF16)
 
     loads[0].wait()
@@ -162,17 +168,12 @@
             xb_one - (jxx * tb_one + jxy * tb_two),
             xb_two - (jxy * tb_one + jyy * tb_two),
         )
-    for peer, dz, dx in [
-        (zt * n_x + lax.rem(x + dx, n_x), zt, dx) for zt in (0, 1, 7, 2, 6, 3, 5, 4) for dx in x_order
-    ]:
+    for peer in [zt * n_x + xt for zt in (0, 1, 7, 2, 6, 3, 5, 4) for xt in (0, 1, 3, 2)]:
         copy = pltpu.make_async_remote_copy(
             src_ref=adj.at[peer], dst_ref=back.at[depth], send_sem=send_sem.at[3],
             recv_sem=back_sem.at[z], device_id=(peer, tile), device_id_type=MESH,
         )
-        if dx:
-            copy.start()
-        else:
-            pl.when(peer != depth)(copy.start)
+        pl.when(peer != depth)(copy.start)
     back[depth] = adj[depth]
 
     settle(id_got.at[pl.ds(0, n_tile - 1)], recv_sem.at[2])
@@ -200,61 +201,64 @@
                 preferred_element_type=F32,
             )
     source = split_two(contrib[...])
-    half = n_tile // 2
     for h in range(2):
         picked = jnp.dot(
-            pick[h * half * 2 * slots:(h + 1) * half * 2 * slots, :], source,
+            pick[h * n_tile * slots:(h + 1) * n_tile * slots, :], source,
             preferred_element_type=F32,
         )
         picked = picked[:, 0:WIDTH] + picked[:, WIDTH:2 * WIDTH]
-        send[h * half:(h + 1) * half] = picked.reshape(half, 2 * slots, WIDTH)
-        for k in range(h * half, min((h + 1) * half, n_tile - 1)):
-            push(send.at[k], got.at[tile], 4, (depth, tile_peers[k]))
-    got[tile] = send[n_tile - 1]
-    settle(got.at[pl.ds(0, n_tile - 1)], recv_sem.at[4])
-
-    both = [
-        split_two(got[:, c * slots:(c + 1) * slots, :].reshape(n_tile * slots, WIDTH))
-        for c in range(2)
-    ]
-    ax, ay = [
-        total[:, 0:WIDTH] + total[:, WIDTH:2 * WIDTH]
-        for total in (jnp.dot(place[...], b, preferred_element_type=F32) for b in both)
-    ]
-    ay_0, ay_1 = ay[0:rows], ay[rows:]
+        send[h] = picked.reshape(n_tile, slots, WIDTH)
+        for k, peer in enumerate(tile_peers):
+            push(send.at[h, k], got.at[h, tile], 4 + h, (depth, peer))
+        got[h, tile] = send[h, n_tile - 1]
+
+    def arrived(h):
+        settle(got.at[h, pl.ds(0, n_tile - 1)], recv_sem.at[4 + h])
+        total = jnp.dot(
+            place[...], split_two(got[h].reshape(n_tile * slots, WIDTH)),
+            preferred_element_type=F32,
+        )
+        total = total[:, 0:WIDTH] + total[:, WIDTH:2 * WIDTH]
+        return total[0:rows], total[rows:]
+
+    before, after = lax.rem(tile + n_tile - 1, n_tile), lax.rem(tile + 1, n_tile)
+    ay_0, ay_1 = arrived(0)
     above = jnp.where(tile == 0, 0.0, -0.5) * ay_0
     below = jnp.where(tile == n_tile - 1, 0.0, 0.5) * ay_1
-    before, after = lax.rem(tile + n_tile - 1, n_tile), lax.rem(tile + 1, n_tile)
-    left, right = neighbours(ax[0:rows])
+    up[0] = smooth(0.25 * above)
+    down[1] = smooth(0.25 * below)
+    push(up.at[0], from_below.at[0], 6, (depth, before))
+    push(down.at[1], from_above.at[1], 7, (depth, after))
+    ax_0, ax_1 = arrived(1)
+    left, right = neighbours(ax_0)
     raw_0 = 0.5 * (left - right) - 0.5 * ay_1
-    up[0] = 0.25 * above
-    up[1] = 0.5 * above + 0.25 * raw_0
-    push(up, from_below, 5, (depth, before))
-    left, right = neighbours(ax[rows:])
+    up[1] = smooth(0.5 * above + 0.25 * raw_0)
+    push(up.at[1], from_below.at[1], 8, (depth, before))
+    left, right = neighbours(ax_1)
     raw_1 = 0.5 * (left - right) + 0.5 * ay_0
-    down[0] = 0.25 * raw_1 + 0.5 * below
-    down[1] = 0.25 * below
-    push(down, from_above, 6, (depth, after))
+    down[0] = smooth(0.25 * raw_1 + 0.5 * below)
+    push(down.at[0], from_above.at[0], 9, (depth, after))
     own = [
-        0.25 * above + 0.5 * raw_0 + 0.25 * raw_1,
-        0.25 * raw_0 + 0.5 * raw_1 + 0.25 * below,
+        smooth(0.25 * above + 0.5 * raw_0 + 0.25 * raw_1),
+        smooth(0.25 * raw_0 + 0.5 * raw_1 + 0.25 * below),
     ]
-    settle(from_below, recv_sem.at[5])
-    settle(from_above, recv_sem.at[6])
+    for kind, ref in enumerate(
+        [from_below.at[0], from_above.at[1], from_below.at[1], from_above.at[0]], 6
+    ):
+        settle(ref, recv_sem.at[kind])
     has_before = jnp.where(tile == 0, 0.0, 1.0)
     has_after = jnp.where(tile == n_tile - 1, 0.0, 1.0)
     for r in range(ROWS):
-        line = own[r] + has_before * from_above[r] + has_after * from_below[r]
-        left, right = neighbours(line)
-        out[:, r, :] = 0.25 * left + 0.5 * line + 0.25 * right
+        out[:, r, :] = own[r] + has_before * from_above[r] + has_after * from_below[r]
 
     settle(scalars.at[pl.ds(0, n_other)], send_sem.at[0])
     settle(planes.at[pl.ds(0, n_other)], send_sem.at[1])
     settle(id_got.at[pl.ds(0, n_tile - 1)], send_sem.at[2])
     settle(back.at[pl.ds(0, n_other)], send_sem.at[3])
-    settle(got.at[pl.ds(0, n_tile - 1)], send_sem.at[4])
-    settle(up, send_sem.at[5])
-    settle(down, send_sem.at[6])
+    for h in range(2):
+        settle(got.at[h, pl.ds(0, n_tile - 1)], send_sem.at[4 + h])
+    for kind, ref in enumerate([up.at[0], down.at[1], up.at[1], down.at[0]], 6):
+        settle(ref, send_sem.at[kind])
 
 
 def per_device(tidal, plane_weight, plane_step, ray_angle, dest_tile, dest_segment, interp):
@@ -293,16 +297,16 @@
             vmem((2 * n_tile * slots, 2 * blocks), BF16),
             vmem((n_tile, 2, blocks), F32),
             vmem((n_tile, 2, blocks), F32),
-            vmem((n_tile, 2 * slots, WIDTH), F32),
-            vmem((n_tile, 2 * slots, WIDTH), F32),
+            vmem((2, n_tile, slots, WIDTH), F32),
+            vmem((2, n_tile, slots, WIDTH), F32),
             vmem((segments, 2 * blocks), BF16),
             vmem((ROWS, rows, WIDTH), F32),
             vmem((ROWS, rows, WIDTH), F32),
             vmem((ROWS, rows, WIDTH), F32),
             vmem((ROWS, rows, WIDTH), F32),
             pltpu.SemaphoreType.DMA((5,)),
-            pltpu.SemaphoreType.DMA((7,)),
-            pltpu.SemaphoreType.DMA((7,)),
+            pltpu.SemaphoreType.DMA((10,)),
+            pltpu.SemaphoreType.DMA((10,)),
             pltpu.SemaphoreType.DMA((n_depth // X_SIZE,)),
         ],
         compiler_params=pltpu.CompilerParams(collective_id=0, vmem_limit_bytes=33554432, has_side_effects=True),

time: 36.3 us -> 36.1 us (level)
  no operation moved by 1% of the time
where the time goes in v4:
time: 36.1 us; the launch traced here: 36 us
  Pallas kernels  34.1 us (94%)
  between operations  1.3 us (4%)
  local copies, waits for them, and re-layouts  0.66 us (2%)
    pallas_call x1, Pallas kernels, per_device(): pl.pallas_call(body, out_shape=jax.ShapeDtypeStruct((rows, ROWS, WIDTH),...  34.1 us

profile of v4, /device:TPU:1, one launch (start us, length us, event | category | flops | bytes accessed | tf_op | source)
XLA Modules:
  0.0 36.0 jit_solution(12518295177018944183)
XLA Ops:
  1.3 34.1 %shard_map.73 = f32[128,2,128]{2,1,0:T(2,128)S(1)} custom-call(f32[3,32,4,128]{3,2,1,0:T(4,128)} %bitcast.9, f32[32,4,128]{2,1,0:T(4,128)} %bitcast.10, bf16[128,128,128]{2,1,0:T(8,128)(2,1)} %bitcast.8, s32[1,128]{1,0:T(1,128)} %bitcast.11, s32[1,128]{1,0:T(1,128)} %refs_4_.1, f32[1]{0:T(128)S(6)} %copy.9.refs_5_, f32[1]{0:T(128)S(6)} %copy.10.refs_6_), custom_call_target="tpu_custom_call" | custom-call | tf_op jit(solution)/shard_map/pallas_call | solution.py:280
  35.4 0.7 %copy.11 = f32[1,2,16384]{2,1,0:T(2,128)} copy(f32[1,2,16384]{2,1,0:T(2,128)S(1)} %bitcast.7) | data formatting | bytes 262144

commit v5 on v4

--- a/solution.py
+++ b/solution.py
@@ -160,14 +160,15 @@
     for plane in range(n_depth - 1, -1, -1):
         s = jnp.broadcast_to(scalars[plane, :, WIDTH // 2:WIDTH // 2 + 1], (lanes, WIDTH))
         jxx, jxy, jyy = planes[plane, 0], planes[plane, 1], planes[plane, 2]
+        cross_term = s * jxy
+        keep_one, keep_two = 1.0 - s * jxx, 1.0 - s * jyy
+        next_one = keep_one * xb_one - cross_term * xb_two - (jxx * tb_one + jxy * tb_two)
+        next_two = keep_two * xb_two - cross_term * xb_one - (jxy * tb_one + jyy * tb_two)
         tb_one = tb_one + s * xb_one
         tb_two = tb_two + s * xb_two
         adj[plane, 0:lanes] = -tb_one
         adj[plane, lanes:2 * lanes] = -tb_two
-        xb_one, xb_two = (
-            xb_one - (jxx * tb_one + jxy * tb_two),
-            xb_two - (jxy * tb_one + jyy * tb_two),
-        )
+        xb_one, xb_two = next_one, next_two
     for peer in [zt * n_x + xt for zt in (0, 1, 7, 2, 6, 3, 5, 4) for xt in (0, 1, 3, 2)]:
         copy = pltpu.make_async_remote_copy(
             src_ref=adj.at[peer], dst_ref=back.at[depth], send_sem=send_sem.at[3],
@@ -227,8 +228,8 @@
     below = jnp.where(tile == n_tile - 1, 0.0, 0.5) * ay_1
     up[0] = smooth(0.25 * above)
     down[1] = smooth(0.25 * below)
+    push(down.at[1], from_above.at[1], 7, (depth, after))
     push(up.at[0], from_below.at[0], 6, (depth, before))
-    push(down.at[1], from_above.at[1], 7, (depth, after))
     ax_0, ax_1 = arrived(1)
     left, right = neighbours(ax_0)
     raw_0 = 0.5 * (left - right) - 0.5 * ay_1

time: 36.1 us -> 36.1 us (level)
  no operation moved by 1% of the time
where the time goes in v5:
time: 36.1 us; the launch traced here: 36 us
  Pallas kernels  34 us (94%)
  between operations  1.3 us (4%)
  local copies, waits for them, and re-layouts  0.66 us (2%)
    pallas_call x1, Pallas kernels, per_device(): pl.pallas_call(body, out_shape=jax.ShapeDtypeStruct((rows, ROWS, WIDTH),...  34 us

profile of v5, /device:TPU:1, one launch (start us, length us, event | category | flops | bytes accessed | tf_op | source)
XLA Modules:
  0.0 36.0 jit_solution(18065260010487963299)
XLA Ops:
  1.3 34.0 %shard_map.73 = f32[128,2,128]{2,1,0:T(2,128)S(1)} custom-call(f32[3,32,4,128]{3,2,1,0:T(4,128)} %bitcast.9, f32[32,4,128]{2,1,0:T(4,128)} %bitcast.10, bf16[128,128,128]{2,1,0:T(8,128)(2,1)} %bitcast.8, s32[1,128]{1,0:T(1,128)} %bitcast.11, s32[1,128]{1,0:T(1,128)} %refs_4_.1, f32[1]{0:T(128)S(6)} %copy.9.refs_5_, f32[1]{0:T(128)S(6)} %copy.10.refs_6_), custom_call_target="tpu_custom_call" | custom-call | tf_op jit(solution)/shard_map/pallas_call | solution.py:281
  35.3 0.7 %copy.11 = f32[1,2,16384]{2,1,0:T(2,128)} copy(f32[1,2,16384]{2,1,0:T(2,128)S(1)} %bitcast.7) | data formatting | bytes 262144
